TPU v7x, 512 devices: a whole 4x8x8 slice. The times are simulated.
512 devices in a mesh: seq: 64 (over z, x, core), head: 8 (over y).
Axes of the slice: x: 4, y: 8, z: 8, core: 2. Of those that a mesh axis runs over, the one named last changes fastest.
Arguments:
- xbc: bfloat16 [24576, 10240], P('seq', 'head'), may hold values from -6 to 6
- gate_z: bfloat16 [24576, 8192], P('seq', 'head'), may hold values from -6 to 6
- dt_raw: bfloat16 [128, 24576], P('head', 'seq'), may hold values from -3 to 3
- dt_bias: float32 [128], P('head'), may hold values from -1 to 0.5
- a_log: float32 [128], P('head'), may hold values from -11.5 to -6.6
- skip_d: float32 [128], P('head'), may hold values from 0.5 to 1.5
- conv_weight: float32 [4, 10240], P(None, 'head'), may hold values from -3 to 3
- conv_bias: float32 [10240], P('head'), may hold values from -3 to 3
- norm_gain: float32 [8192], P('head'), may hold values from 0.1 to 1.9
- out_weight: bfloat16 [8192, 4096], P('head', 'seq'), may hold values from -0.1875 to 0.1875
- starts: int32 [24576], P('seq'), may hold values from 0 to 1, as said below
Outputs:
- mixed: bfloat16 [24576, 4096], P('seq', 'head')
Inputs may be any that keep to these rules, and one draw needn't show every extreme that they name: `starts`: a 0 or 1 flag for every token; every 1 lies among the first 6144 tokens, and there is at least one.
All inputs are finite; a program needn't handle non-finite values.
Results may differ from a plain program's by a relative error of at most 0.013.
Values may be sent and summed in bfloat16 or wider, within the bound.
A program may use at most 128 MiB of HBM per device.

v0:
```python
import jax
import jax.numpy as jnp
from jax import lax
from jax.sharding import PartitionSpec as P

P_SIZE = 64
N = 128
DI = 8192
HG = 16
GW = 1280


def carried_in(part, axis, combine, identity):
    place = lax.axis_index(axis)
    gathered = jax.tree.map(lambda a: lax.all_gather(a, axis), part)
    state = jax.tree.map(lambda a, e: jnp.zeros_like(a) + jnp.asarray(e, a.dtype), part, identity)

    def one(hop, state):
        return combine(
            state, jax.tree.map(lambda a: lax.dynamic_index_in_dim(a, hop, 0, False), gathered)
        )

    return lax.fori_loop(0, place, one, state)


def passed_along(block, axis, distance):
    devices = range(lax.axis_size(axis))
    route = [(i - distance, i) for i in devices if i - distance in devices]
    return lax.ppermute(block, axis, route)


def combine(earlier, later):
    return (earlier[0] * later[0], later[0][:, None, None] * earlier[1] + later[1])


def chain_states(decays, states):
    identity = (jnp.ones_like(decays), jnp.zeros_like(states))
    result = carried_in((decays, states), "seq", combine, identity)
    return result[1]


def block_local(item):
    xc, bc, cc, dtc, lc, sc = item
    cumul = jnp.cumsum(lc, axis=1)
    runs = jnp.cumsum(sc)
    tail = (
        jnp.where(
            (runs == runs[-1])[None, :], jnp.exp(jnp.minimum(cumul[:, -1:] - cumul, 0.0)), 0.0
        )
        * dtc
    )
    b_heads = jnp.repeat(bc, HG, axis=1)
    scaled = (tail[:, :, None] * jnp.swapaxes(b_heads, 0, 1).astype(jnp.float32)).astype(
        jnp.bfloat16
    )
    local = jnp.einsum("shp,hsn->hpn", xc, scaled, preferred_element_type=jnp.float32)
    total = jnp.exp(cumul[:, -1]) * (runs[-1] == 0).astype(jnp.float32)
    enter = jnp.exp(cumul) * (runs == 0).astype(jnp.float32)[None, :]
    return (local, total, enter)


def block_inner(item):
    xc, bc, cc, dtc, lc, sc = item
    length = xc.shape[0]
    cumul = jnp.cumsum(lc, axis=1)
    runs = jnp.cumsum(sc)
    lower = jnp.arange(length)[:, None] >= jnp.arange(length)[None, :]
    same = lower & (runs[:, None] == runs[None, :])
    diff = cumul[:, :, None] - cumul[:, None, :]
    wdec = jnp.where(same[None], jnp.exp(jnp.minimum(diff, 0.0)), 0.0)
    scores = jnp.einsum("tgn,sgn->gts", cc, bc, preferred_element_type=jnp.float32)
    scores_h = jnp.repeat(scores, HG, axis=0)
    weights = (scores_h * wdec * dtc[:, None, :]).astype(jnp.bfloat16)
    return jnp.einsum("hts,shp->thp", weights, xc, preferred_element_type=jnp.float32)


def body(
    xbc,
    gate_z,
    dt_raw,
    dt_bias,
    a_log,
    skip_d,
    conv_weight,
    conv_bias,
    norm_gain,
    out_weight,
    starts,
):
    tok = xbc.shape[0]
    width = conv_weight.shape[0]
    chans = xbc.shape[1]
    groups = chans // GW
    heads = dt_raw.shape[0]
    rim, rim_flags = passed_along(
        (xbc[tok - (width - 1) :], starts[tok - (width - 1) :].astype(jnp.bfloat16)), "seq", 1
    )
    flags_int = rim_flags.astype(jnp.int32)
    after_rim = jnp.sum(flags_int) - jnp.cumsum(flags_int)
    counts = jnp.cumsum(starts)
    padded = jnp.concatenate([rim, xbc], axis=0).astype(jnp.float32)
    count_ext = jnp.concatenate([-after_rim, counts])
    acc = conv_bias[None, :] + conv_weight[width - 1][None, :] * xbc.astype(jnp.float32)
    for lag in range(1, width):
        shifted = padded[width - 1 - lag : width - 1 - lag + tok]
        keep = (count_ext[width - 1 - lag : width - 1 - lag + tok] == counts).astype(jnp.float32)
        acc = acc + conv_weight[width - 1 - lag][None, :] * shifted * keep[:, None]
    unit = jax.nn.silu(acc).astype(jnp.bfloat16)
    grid = unit.reshape(tok, groups, GW)
    xs = grid[:, :, : HG * P_SIZE].reshape(tok, heads, P_SIZE)
    bmat = grid[:, :, HG * P_SIZE : HG * P_SIZE + N]
    cmat = grid[:, :, HG * P_SIZE + N :]
    steps_dt = jax.nn.softplus(dt_raw.astype(jnp.float32) + dt_bias[:, None])
    logs = -jnp.exp(a_log)[:, None] * steps_dt
    length = min(128, tok)
    nblocks = tok // length
    x_blocks = xs.reshape(nblocks, length, heads, P_SIZE)
    b_blocks = bmat.reshape(nblocks, length, groups, N)
    c_blocks = cmat.reshape(nblocks, length, groups, N)
    dt_blocks = steps_dt.reshape(heads, nblocks, length).transpose(1, 0, 2)
    log_blocks = logs.reshape(heads, nblocks, length).transpose(1, 0, 2)
    start_blocks = starts.reshape(nblocks, length)
    items = (x_blocks, b_blocks, c_blocks, dt_blocks, log_blocks, start_blocks)

    def fold(carry, item):
        local, total = item
        return ((carry[0] * total, carry[1] * total[:, None, None] + local), None)

    y_diag, (locals_all, totals, enters) = lax.map(
        lambda item: (block_inner(item), block_local(item)), items
    )
    init = (jnp.ones((heads,), jnp.float32), jnp.zeros((heads, P_SIZE, N), jnp.float32))
    result, unused = lax.scan(fold, init, (locals_all, totals))
    entering = chain_states(result[0], result[1])

    def apply(state, item):
        cc, enter, local, total = item
        c_heads = jnp.repeat(cc, HG, axis=1)
        y_off = (
            jnp.einsum(
                "thn,hpn->thp",
                c_heads,
                state.astype(jnp.bfloat16),
                preferred_element_type=jnp.float32,
            )
            * enter.T[:, :, None]
        )
        return (state * total[:, None, None] + local, y_off)

    unused_state, y_offs = lax.scan(apply, entering, (c_blocks, enters, locals_all, totals))
    y_all = (y_diag + y_offs).reshape(tok, heads, P_SIZE) + skip_d[None, :, None] * xs.astype(
        jnp.float32
    )
    gated = y_all.reshape(tok, heads * P_SIZE) * jax.nn.silu(gate_z.astype(jnp.float32))
    total_sq = lax.psum(jnp.sum(gated * gated, axis=1), "head")
    normed = (gated * lax.rsqrt(total_sq / DI + 1e-05)[:, None] * norm_gain[None, :]).astype(
        jnp.bfloat16
    )
    terms = jnp.dot(
        normed,
        lax.all_gather(out_weight, "seq", axis=1, tiled=True),
        preferred_element_type=jnp.float32,
    )
    return lax.psum_scatter(terms.astype(jnp.bfloat16), "head", scatter_dimension=1, tiled=True)


def solution(mesh):
    placed = (
        P("seq", "head"),
        P("seq", "head"),
        P("head", "seq"),
        P("head"),
        P("head"),
        P("head"),
        P(None, "head"),
        P("head"),
        P("head"),
        P("head", "seq"),
        P("seq"),
    )
    return jax.shard_map(
        body, mesh=mesh, in_specs=placed, out_specs=P("seq", "head"), check_vma=False
    )
```

profile of v0, /device:TPU:1, one launch (start us, length us, event | category | flops | bytes accessed | tf_op | source)
XLA Modules:
  0.0 366.4 jit_solution(15041050396364430548)
XLA Ops:
  7.3 4.5 %collective-permute-start.1 = (bf16[3]{0:T(256)(128)(2,1)S(1)}, bf16[3]{0:T(256)(128)(2,1)S(1)}, u32[]{:S(2)}, u32[]{:S(2)}) collective-permute-start(bf16[3]{0:T(256)(128)(2,1)S(1)} %slice.68), channel_id=1, source_target_pairs={{0,8},{8,16},{16,24},{24,32},{32,40},{40,48},{48,56},{56,64},{64,7... | collective-permute-start | bytes 26 | tf_op jit(solution)/shard_map/ppermute | solution.py:29
  12.5 1.9 collective-permute-start
  14.5 1.0 reduce-window.22
  15.8 0.9 slice_reduce_fusion.4
  20.0 1.4 maximum_convert_fusion
  21.5 1.9 fusion.44
  23.4 0.9 copy-done.1
  24.3 1.9 reshape.277
  26.2 2.0 copy.38
  28.2 1.3 broadcast.139.clone
  29.5 17.6 %while.53 = (s32[]{:T(128)}, f32[3,128,16,64]{1,3,2,0:T(8,128)}, f32[3,16,64,128]{3,2,1,0:T(8,128)S(1)}, f32[3,16]{1,0:T(4,128)S(1)}, f32[3,16,128]{2,1,0:T(8,12...) while((s32[]{:T(128)}, f32[3,128,16,64]{1,3,2,0:T(8,128)}, ...), condition=%wide.region_7.8_spmd, body=%wide.region_4.7_spmd.sunk | while | flops 73752848 | bytes 2099011 | solution.py:129
  34.0 1.4 fusion.75
  39.9 1.4 fusion.75
  45.7 1.4 fusion.75
  49.4 1.3 dynamic-slice
  51.7 132.0 %all-reduce = f32[1024]{0:T(1024)S(1)} all-reduce(f32[1024]{0:T(1024)S(1)} %dynamic-update-slice), channel_id=2, replica_groups=mesh['seq'=64,'head'=8] {'seq'}, use_global_device_ids=true, to_apply=%add | all-reduce | flops 1024 | bytes 8192
  183.8 18.0 %all-gather.7.cloned.1.call-done = f32[1024,64,128]{2,1,0:T(8,128)} async-done(((f32[16,64,128]{2,1,0:T(8,128)}), f32[1024,64,128]{2,1,0:T(8,128)}) %all-gather.7.cloned.1.call-update) | async-done | bytes 33554448 | tf_op jit(solution)/shard_map/all_gather | solution.py:15
  201.8 1.2 while.54
  201.8 1.2 bitcast_add_fusion.6
  203.0 1.3 broadcast.139
  204.4 4.4 %while.55 = (s32[]{:T(128)}, f32[16,64,128]{2,1,0:T(8,128)S(1)}, f32[3,128,16,64]{1,3,2,0:T(8,128)}, f32[3,16]{1,0:T(4,128)S(1)}, f32[3,16,64,128]{3,2,1,0:T(8,1...) while((s32[]{:T(128)}, f32[16,64,128]{2,1,0:T(8,128)S(1)}, ...), condition=%wide.region_13.14_spmd, body=%wide.region_12.13_spmd.sunk | while | flops 34078720 | bytes 2745125 | solution.py:150
  204.4 1.3 fusion.81
  205.9 1.3 fusion.81
  207.3 1.3 fusion.81
  208.8 3.4 add.93
  212.2 2.3 copy.48
  214.5 1.8 reshape.278
  216.3 2.6 multiply_reduce_fusion.1
  218.9 13.3 %psum.7 = f32[384]{0:T(512)S(1)} all-reduce(f32[384]{0:T(512)S(1)} %get-tuple-element.329), channel_id=1, replica_groups=mesh['seq'=64,'head'=8] {'head'}, use_global_device_ids=true, to_apply=%region_15.16 | all-reduce | flops 384 | bytes 3072 | tf_op jit(solution)/shard_map/psum | solution.py:155
  232.2 58.5 %all-gather.5.cloned.1.call-done = bf16[1024,4096]{0,1:T(8,128)(2,1)} async-done(((bf16[1024,64]{0,1:T(8,128)(2,1)}), bf16[1024,4096]{0,1:T(8,128)(2,1)}) %all-gather.5.cloned.1.call-update) | async-done | bytes 8388624 | tf_op jit(solution)/shard_map/all_gather | solution.py:161
  290.7 10.2 %convolution_convert_fusion = bf16[384,4096]{1,0:T(8,128)(2,1)} fusion(bf16[1024,4096]{0,1:T(8,128)(2,1)} %all-gather.5.cloned.1.call-done, f32[384,1024]{1,0:T(8,128)S(1)} %get-tuple-element.330, f32[1024]{0:T(1024)S(1)} %copy-done.5, f32[384]{0:T(512)S(1)} %add_rsqrt_fusion), kind=kOutput, calls=%fused_computation.59 | convolution fusion | flops 3223977984 | bytes 13112832 | tf_op jit(solution)/shard_map/dot_general | solution.py:159
  300.9 59.0 %reduce-scatter.2.cloned.1.call-done = bf16[384,512]{1,0:T(8,128)(2,1)} async-done(((bf16[384,4096]{1,0:T(8,128)(2,1)}), bf16[384,512]{1,0:T(8,128)(2,1)}) %reduce-scatter.2.cloned.1.call-update) | async-done | bytes 393232 | tf_op jit(solution)/shard_map/reduce_scatter | solution.py:164
  (118 shorter events, 19.9 us)
Async XLA Ops:
  6.5 195.2 %all-gather.7.cloned.1.call-start = ((), (), s32[]{:S(2)}) async-start(), calls=%async_computation.3 | async-start | bytes 34078720 | tf_op jit(solution)/shard_map/all_gather | solution.py:15
  7.3 11.0 %collective-permute-start.1 = (bf16[3]{0:T(256)(128)(2,1)S(1)}, bf16[3]{0:T(256)(128)(2,1)S(1)}, u32[]{:S(2)}, u32[]{:S(2)}) collective-permute-start(bf16[3]{0:T(256)(128)(2,1)S(1)} %slice.68), channel_id=1, source_target_pairs={{0,8},{8,16},{16,24},{24,32},{32,40},{40,48},{48,56},{56,64},{64,7... | collective-permute-start | bytes 26 | tf_op jit(solution)/shard_map/ppermute | solution.py:29
  12.5 7.5 %collective-permute-start = (bf16[3,1280]{1,0:T(4,128)(2,1)S(1)}, bf16[3,1280]{1,0:T(4,128)(2,1)S(1)}, u32[]{:S(2)}, u32[]{:S(2)}) collective-permute-start(bf16[3,1280]{1,0:T(4,128)(2,1)S(1)} %slice.66), channel_id=1, source_target_pairs={{0,8},{8,16},{16,24},{24,32},{32,40},{40,48},{48,56},{56,64},{64,7... | collective-permute-start | bytes 23048 | tf_op jit(solution)/shard_map/ppermute | solution.py:29
  18.2 3.2 copy-start.2
  18.2 3.2 copy-start.3
  23.3 1.0 copy-start.1
  47.1 2.1 copy-start.4
  47.6 0.8 copy-start
  48.5 242.3 %all-gather.5.cloned.1.call-start = ((), (), s32[]{:S(2)}) async-start(), calls=%async_computation.1 | async-start | bytes 8519680 | tf_op jit(solution)/shard_map/all_gather | solution.py:161
  49.2 310.7 %reduce-scatter.2.cloned.1.call-start = ((), (), s32[]{:S(2)}) async-start(), calls=%async_computation.2 | async-start | bytes 3538944 | tf_op jit(solution)/shard_map/reduce_scatter | solution.py:164
  216.3 74.4 %copy-start.5 = (f32[1024]{0:T(1024)S(1)}, f32[1024]{0:T(1024)}, u32[]{:S(2)}) copy-start(f32[1024]{0:T(1024)} %param.27) | copy-start | bytes 12292
Sparse Core Ops, SparseCore 0:
  48.6 153.1 all-gather.6
  205.1 85.5 all-gather.4
  301.1 58.8 reduce-scatter.1
where the time goes:
time: 372 us; the launch traced here: 366 us
  blocking collectives  145 us (39%)
  waiting for transfers between devices  136 us (37%)
  other arithmetic  21.2 us (6%)
  local copies, waits for them, and re-layouts  20.7 us (6%)
  matrix products  20.1 us (5%)
  between operations  14 us (4%)
  starting transfers between devices  6.48 us (2%)
    unnamed x1, blocking collectives  132 us
    reduce_scatter x1, waiting for transfers between devices, body(): lax.psum_scatter(terms.astype(jnp.bfloat16), 'head', scatter_dimension=1,...  59 us
    all_gather x1, waiting for transfers between devices, body(): lax.all_gather(out_weight, 'seq', axis=1, tiled=True)  58.5 us
    all_gather x1, waiting for transfers between devices, carried_in(): gathered = jax.tree.map(lambda a: lax.all_gather(a, axis), part)  18 us
    psum x1, blocking collectives, body(): total_sq = lax.psum(jnp.sum(gated * gated, axis=1), 'head')  13.3 us
    dot_general x1, matrix products, body(): jnp.dot(normed, lax.all_gather(out_weight, 'seq', axis=1, tiled=True), pr...  10.2 us
  transfers between devices with their start and end apart: 5, of which 3 were waited for; matrix products, arithmetic and copies ran while one was open for 7% of the time, Pallas kernels for 0%

commit v1 on v0

--- a/solution.py
+++ b/solution.py
@@ -1,6 +1,8 @@
 import jax
 import jax.numpy as jnp
 from jax import lax
+from jax.experimental import pallas as pl
+from jax.experimental.pallas import tpu as pltpu
 from jax.sharding import PartitionSpec as P
 
 P_SIZE = 64
@@ -10,33 +12,125 @@
 GW = 1280
 
 
-def carried_in(part, axis, combine, identity):
-    place = lax.axis_index(axis)
-    gathered = jax.tree.map(lambda a: lax.all_gather(a, axis), part)
-    state = jax.tree.map(lambda a, e: jnp.zeros_like(a) + jnp.asarray(e, a.dtype), part, identity)
-
-    def one(hop, state):
-        return combine(
-            state, jax.tree.map(lambda a: lax.dynamic_index_in_dim(a, hop, 0, False), gathered)
-        )
-
-    return lax.fori_loop(0, place, one, state)
-
-
 def passed_along(block, axis, distance):
     devices = range(lax.axis_size(axis))
     route = [(i - distance, i) for i in devices if i - distance in devices]
     return lax.ppermute(block, axis, route)
 
 
-def combine(earlier, later):
-    return (earlier[0] * later[0], later[0][:, None, None] * earlier[1] + later[1])
+MESH = pl.DeviceIdType.MESH
+ROW = 8
+
+
+def decay_of(tile):
+    both = tile.astype(jnp.float32)
+    return both[0:1] + both[8:9]
+
+
+def states_kernel(
+    mine_ref, out_ref, row_buf, total_buf, column_buf, back_buf, land_buf, s1, r1, s2, r2, s3, r3
+):
+    place = lax.axis_index("seq")
+    z = place // ROW
+    j = place % ROW
+    row_peers = [(j + k) % ROW for k in range(1, ROW)]
+    column_peers = [(z + k) % ROW for k in range(1, ROW)]
+    barrier = pltpu.get_barrier_semaphore()
+    for peer in row_peers:
+        pl.semaphore_signal(barrier, 1, device_id={"seq": z * ROW + peer}, device_id_type=MESH)
+    for peer in column_peers:
+        pl.semaphore_signal(barrier, 1, device_id={"seq": peer * ROW + j}, device_id_type=MESH)
+    pl.semaphore_wait(barrier, 2 * (ROW - 1))
+    copies = []
+    for k, peer in enumerate(row_peers):
+        copies.append(
+            pltpu.make_async_remote_copy(
+                mine_ref.at[peer], row_buf.at[j], s1.at[k], r1.at[k],
+                device_id={"seq": z * ROW + peer}, device_id_type=MESH,
+            )
+        )
+        copies[-1].start()
+    row_buf[j] = mine_ref[j]
+    for copy in copies:
+        copy.wait()
+    for head in range(2):
+        total = row_buf[0, head, :P_SIZE].astype(jnp.float32)
+        decay = decay_of(row_buf[0, head, P_SIZE:])
+        for i in range(1, ROW):
+            one = decay_of(row_buf[i, head, P_SIZE:])
+            total = total * one + row_buf[i, head, :P_SIZE].astype(jnp.float32)
+            decay = decay * one
+        total_buf[head, :P_SIZE] = total.astype(jnp.bfloat16)
+        high = decay.astype(jnp.bfloat16)
+        low = decay - high.astype(jnp.float32)
+        pair = jnp.concatenate(
+            [jnp.broadcast_to(high.astype(jnp.float32), (8, N)), jnp.broadcast_to(low, (8, N))], axis=0
+        )
+        total_buf[head, P_SIZE:] = pair.astype(jnp.bfloat16)
+    copies = []
+    for k, peer in enumerate(column_peers):
+        copies.append(
+            pltpu.make_async_remote_copy(
+                total_buf, column_buf.at[z], s2.at[k], r2.at[k],
+                device_id={"seq": peer * ROW + j}, device_id_type=MESH,
+            )
+        )
+        copies[-1].start()
+    column_buf[z] = total_buf[...]
+    for copy in copies:
+        copy.wait()
+    for head in range(2):
+        state = jnp.zeros((P_SIZE, N), jnp.float32)
+        for i in range(ROW - 1):
+            one = decay_of(column_buf[i, head, P_SIZE:])
+            after = state * one + column_buf[i, head, :P_SIZE].astype(jnp.float32)
+            state = jnp.where(i < z, after, state)
+        for i in range(ROW):
+            back_buf[i, head] = state.astype(jnp.bfloat16)
+            if i < ROW - 1:
+                one = decay_of(row_buf[i, head, P_SIZE:])
+                state = state * one + row_buf[i, head, :P_SIZE].astype(jnp.float32)
+    copies = []
+    for k, peer in enumerate(row_peers):
+        copies.append(
+            pltpu.make_async_remote_copy(
+                back_buf.at[peer], land_buf.at[j], s3.at[k], r3.at[k],
+                device_id={"seq": z * ROW + peer}, device_id_type=MESH,
+            )
+        )
+        copies[-1].start()
+    land_buf[j] = back_buf[j]
+    for copy in copies:
+        copy.wait()
+    out_ref[...] = land_buf[...]
 
 
 def chain_states(decays, states):
-    identity = (jnp.ones_like(decays), jnp.zeros_like(states))
-    result = carried_in((decays, states), "seq", combine, identity)
-    return result[1]
+    high = lax.reduce_precision(decays, 8, 7)
+    pair = jnp.stack([high, decays - high], axis=1)
+    rows = jnp.broadcast_to(
+        pair[:, :, None, None], (HG, 2, 8, N)
+    ).reshape(HG, 16, N)
+    mine = jnp.concatenate([states, rows], axis=1).astype(jnp.bfloat16)
+    part = P_SIZE + 16
+    entering = pl.pallas_call(
+        states_kernel,
+        out_shape=jax.ShapeDtypeStruct((ROW, 2, P_SIZE, N), jnp.bfloat16),
+        in_specs=[pl.BlockSpec(memory_space=pltpu.VMEM)],
+        out_specs=pl.BlockSpec(memory_space=pltpu.VMEM),
+        scratch_shapes=[
+            pltpu.VMEM((ROW, 2, part, N), jnp.bfloat16),
+            pltpu.VMEM((2, part, N), jnp.bfloat16),
+            pltpu.VMEM((ROW, 2, part, N), jnp.bfloat16),
+            pltpu.VMEM((ROW, 2, P_SIZE, N), jnp.bfloat16),
+            pltpu.VMEM((ROW, 2, P_SIZE, N), jnp.bfloat16),
+        ]
+        + [pltpu.SemaphoreType.DMA((ROW - 1,))] * 6,
+        compiler_params=pltpu.CompilerParams(collective_id=0, has_side_effects=True),
+        cost_estimate=pl.CostEstimate(flops=10**7, bytes_accessed=10**6, transcendentals=0),
+        name="chain_states",
+    )(mine.reshape(ROW, 2, part, N))
+    return entering.reshape(HG, P_SIZE, N).astype(jnp.float32)
 
 
 def block_local(item):

time: 372 us -> 196 us (0.53)
  blocking collectives: 145 us -> 13.6 us
  waiting for transfers between devices: 136 us -> 46.8 us
  Pallas kernels: 0 us -> 40.3 us
  matrix products: 20.1 us -> 26 us
    unnamed x1 -> x0, blocking collectives: 132 us -> none
    all_gather x1, waiting for transfers between devices: 58.5 us -> 0.01 us  [body(): lax.all_gather(out_weight, 'seq', axis=1, tiled=True)]
    pallas_call x0 -> x1, Pallas kernels: none -> 40.3 us  [chain_states(): pl.pallas_call(states_kernel, out_shape=jax.ShapeDtypeStruct((ROW, 2, P_S...]
    all_gather x1 -> x0, waiting for transfers between devices: 18 us -> none  [carried_in(): gathered = jax.tree.map(lambda a: lax.all_gather(a, axis), part)]
    reduce_scatter x1, waiting for transfers between devices: 59 us -> 46.1 us  [body(): lax.psum_scatter(terms.astype(jnp.bfloat16), 'head', scatter_dimension=1,...]
  transfers between devices with their start and end apart: 5 -> 4, of which waited for: 3 -> 1; matrix products, arithmetic and copies ran while one was open for 7% -> 31% of each run, Pallas kernels for 0% -> 21%
where the time goes in v1:
time: 196 us; the launch traced here: 192 us
  waiting for transfers between devices  46.8 us (24%)
  Pallas kernels  40.3 us (21%)
  matrix products  26 us (13%)
  other arithmetic  22.3 us (11%)
  local copies, waits for them, and re-layouts  21.2 us (11%)
  blocking collectives  13.6 us (7%)
  between operations  13.6 us (7%)
  starting transfers between devices  6.43 us (3%)
  loops' own time  2.19 us (1%)
    reduce_scatter x1, waiting for transfers between devices, body(): lax.psum_scatter(terms.astype(jnp.bfloat16), 'head', scatter_dimension=1,...  46.1 us
    pallas_call x1, Pallas kernels, chain_states(): pl.pallas_call(states_kernel, out_shape=jax.ShapeDtypeStruct((ROW, 2, P_S...  40.3 us
    psum x1, blocking collectives, body(): total_sq = lax.psum(jnp.sum(gated * gated, axis=1), 'head')  13.6 us
    dot_general x1, matrix products, body(): jnp.dot(normed, lax.all_gather(out_weight, 'seq', axis=1, tiled=True), pr...  10.2 us
    dot_general x3, matrix products, block_inner(): jnp.einsum('hts,shp->thp', weights, xc, preferred_element_type=jnp.float32)  7.01 us
    ppermute x2, starting transfers between devices, passed_along(): return lax.ppermute(block, axis, route)  6.39 us
    dot_general x3, matrix products, block_local(): jnp.einsum('shp,hsn->hpn', xc, scaled, preferred_element_type=jnp.float32)  4.45 us
    reshape x2, local copies, waits for them, and re-layouts, body(): (y_diag + y_offs).reshape(tok, heads, P_SIZE)  4.1 us
  transfers between devices with their start and end apart: 4, of which 1 were waited for; matrix products, arithmetic and copies ran while one was open for 31% of the time, Pallas kernels for 21%

profile of v1, /device:TPU:1, one launch (start us, length us, event | category | flops | bytes accessed | tf_op | source)
XLA Modules:
  0.0 192.5 jit_solution(5480957932395447343)
XLA Ops:
  8.1 4.5 %collective-permute-start.1 = (bf16[3]{0:T(256)(128)(2,1)S(1)}, bf16[3]{0:T(256)(128)(2,1)S(1)}, u32[]{:S(2)}, u32[]{:S(2)}) collective-permute-start(bf16[3]{0:T(256)(128)(2,1)S(1)} %slice.68), channel_id=1, source_target_pairs={{0,8},{8,16},{16,24},{24,32},{32,40},{40,48},{48,56},{56,64},{64,7... | collective-permute-start | bytes 26 | tf_op jit(solution)/shard_map/ppermute | solution.py:18
  13.3 1.9 collective-permute-start
  15.3 1.0 reduce-window.22
  17.0 0.8 compare_select_fusion
  18.8 0.9 slice_reduce_fusion.4
  21.3 1.4 maximum_convert_fusion
  22.8 2.8 %fusion.44 = bf16[384,1,1280]{2,0,1:T(8,128)(2,1)S(1)} fusion(f32[384]{0:T(512)S(1)} %get-tuple-element.267, f32[387,1280]{1,0:T(8,128)S(1)} %maximum_convert_fusion, f32[1280]{0:T(1024)S(1)} %get-tuple-element.206, f32[384]{0:T(512)S(1)} %get-tuple-element.268, f32[1280]{0:T(1024)S(1)} %get-tuple-element.207, f32[384]{0:T(512)S(1)} %get-tuple-element.266, ...), kind=kLoop, calls=%fused_computation.79 | loop fusion | flops 8355840 | bytes 7894528 | tf_op jit(solution)/shard_map/reshape | solution.py:203
  25.6 1.1 slice.86
  26.7 3.2 %reshape.282 = bf16[3,128,16,64]{3,2,1,0:T(8,128)(2,1)} reshape(bf16[384,1,1024]{2,0,1:T(8,128)(2,1)} %slice.86) | data formatting | bytes 1572864 | tf_op jit(solution)/shard_map/reshape;reshape | solution.py:211
  29.9 2.6 %copy.30 = bf16[3,128,16,64]{1,3,2,0:T(8,128)(2,1)} copy(bf16[3,128,16,64]{3,2,1,0:T(8,128)(2,1)} %reshape.282) | data formatting | bytes 1572864 | tf_op jit(solution)/shard_map/while | solution.py:223
  32.5 1.4 broadcast.141.clone
  33.9 22.8 %while.41 = (s32[]{:T(128)}, f32[3,128,16,64]{1,3,2,0:T(8,128)}, f32[3,16,64,128]{3,2,1,0:T(8,128)S(1)}, f32[3,16]{1,0:T(4,128)S(1)}, f32[3,16,128]{2,1,0:T(8,12...) while((s32[]{:T(128)}, f32[3,128,16,64]{1,3,2,0:T(8,128)}, ...), condition=%wide.region_7.8_spmd, body=%wide.region_4.7_spmd.sunk | while | flops 73752848 | bytes 2099011 | solution.py:223
  37.4 1.5 fusion.77
  39.2 2.3 %fusion.76 = f32[3,128,16,64]{1,3,2,0:T(8,128)} fusion(f32[3,128,16,64]{1,3,2,0:T(8,128)} %get-tuple-element.443, s32[]{:T(128)} %get-tuple-element.442, f32[16,128]{1,0:T(8,128)S(1)} %bitcast.142, f32[16,128]{1,0:T(8,128)S(1)} %reduce_window_sum.46, f32[128,128]{1,0:T(8,128)S(1)} %fusion.73, pred[128,128]{1,0:T(8,128)(4,1)S(1)} %fusion.75, ...), kind=kOutput, calls=%fused_computation.19.clone.1 | convolution fusion | flops 35127296 | bytes 893952 | tf_op jit(solution)/shard_map/while/body/eval_jaxpr/hts,shp->thp/dot_general | solution.py:168
  45.0 1.5 fusion.77
  46.7 2.3 %fusion.76 = f32[3,128,16,64]{1,3,2,0:T(8,128)} fusion(f32[3,128,16,64]{1,3,2,0:T(8,128)} %get-tuple-element.443, s32[]{:T(128)} %get-tuple-element.442, f32[16,128]{1,0:T(8,128)S(1)} %bitcast.142, f32[16,128]{1,0:T(8,128)S(1)} %reduce_window_sum.46, f32[128,128]{1,0:T(8,128)S(1)} %fusion.73, pred[128,128]{1,0:T(8,128)(4,1)S(1)} %fusion.75, ...), kind=kOutput, calls=%fused_computation.19.clone.1 | convolution fusion | flops 35127296 | bytes 893952 | tf_op jit(solution)/shard_map/while/body/eval_jaxpr/hts,shp->thp/dot_general | solution.py:168
  52.6 1.5 fusion.77
  54.4 2.4 %fusion.76 = f32[3,128,16,64]{1,3,2,0:T(8,128)} fusion(f32[3,128,16,64]{1,3,2,0:T(8,128)} %get-tuple-element.443, s32[]{:T(128)} %get-tuple-element.442, f32[16,128]{1,0:T(8,128)S(1)} %bitcast.142, f32[16,128]{1,0:T(8,128)S(1)} %reduce_window_sum.46, f32[128,128]{1,0:T(8,128)S(1)} %fusion.73, pred[128,128]{1,0:T(8,128)(4,1)S(1)} %fusion.75, ...), kind=kOutput, calls=%fused_computation.19.clone.1 | convolution fusion | flops 35127296 | bytes 893952 | tf_op jit(solution)/shard_map/while/body/eval_jaxpr/hts,shp->thp/dot_general | solution.py:168
  58.4 40.3 %chain_states.1 = bf16[8,2,64,128]{3,2,1,0:T(8,128)(2,1)} custom-call(bf16[8,2,80,128]{3,2,1,0:T(8,128)(2,1)} %pad_maximum_fusion.mine_ref), custom_call_target="tpu_custom_call" | custom-call | flops 10000000 | bytes 1000000 | tf_op jit(solution)/shard_map/chain_states/pallas_call | solution.py:116
  98.7 1.0 bitcast_convert_fusion.1
  99.7 1.4 broadcast.141
  101.2 4.5 %while.42 = (s32[]{:T(128)}, f32[16,64,128]{2,1,0:T(8,128)S(1)}, f32[3,128,16,64]{1,3,2,0:T(8,128)}, f32[3,16]{1,0:T(4,128)S(1)}, f32[3,16,64,128]{3,2,1,0:T(8,1...) while((s32[]{:T(128)}, f32[16,64,128]{2,1,0:T(8,128)S(1)}, ...), condition=%wide.region_11.12_spmd, body=%wide.region_10.11_spmd.sunk | while | flops 34078720 | bytes 2745125 | solution.py:244
  101.2 1.3 fusion.82
  102.7 1.3 fusion.82
  104.2 1.3 fusion.82
  105.7 3.4 %add.78 = f32[3,128,16,64]{1,3,2,0:T(8,128)} add(f32[3,128,16,64]{1,3,2,0:T(8,128)} %get-tuple-element.130, f32[3,128,16,64]{1,3,2,0:T(8,128)} %get-tuple-element.136) | non-fusion elementwise | flops 393216 | bytes 4718592 | tf_op jit(solution)/shard_map/add | solution.py:245
  109.1 2.3 %copy.41 = f32[3,128,16,64]{3,2,1,0:T(8,128)S(1)} copy(f32[3,128,16,64]{1,3,2,0:T(8,128)} %add.78) | data formatting | bytes 3145728 | tf_op jit(solution)/shard_map/reshape | solution.py:245
  111.3 1.8 reshape.283
  113.2 2.5 %multiply_reduce_fusion.1 = (f32[384]{0:T(512)S(1)}, f32[384,1024]{1,0:T(8,128)S(1)}) fusion(bf16[384,1024]{1,0:T(8,128)(2,1)} %param.18, f32[384,1024]{1,0:T(8,128)} %reshape.283, bf16[384,1,1280]{2,0,1:T(8,128)(2,1)} %copy-done, f32[1024]{0:T(1024)S(1)} %mul.225), kind=kLoop, calls=%fused_computation.77 | loop fusion | flops 4324992 | bytes 4724224 | tf_op jit(solution)/shard_map/reduce_sum | solution.py:249
  115.7 13.6 %psum.7 = f32[384]{0:T(512)S(1)} all-reduce(f32[384]{0:T(512)S(1)} %get-tuple-element.256), channel_id=1, replica_groups=mesh['seq'=64,'head'=8] {'head'}, use_global_device_ids=true, to_apply=%region_13.14 | all-reduce | flops 384 | bytes 3072 | tf_op jit(solution)/shard_map/psum | solution.py:249
  129.3 10.2 %convolution_convert_fusion = bf16[384,4096]{1,0:T(8,128)(2,1)} fusion(bf16[1024,4096]{0,1:T(8,128)(2,1)} %all-gather.2.cloned.1.call-done, f32[384,1024]{1,0:T(8,128)S(1)} %get-tuple-element.257, f32[1024]{0:T(1024)S(1)} %copy-done.2, f32[384]{0:T(512)S(1)} %add_rsqrt_fusion), kind=kOutput, calls=%fused_computation.57 | convolution fusion | flops 3223977984 | bytes 13112832 | tf_op jit(solution)/shard_map/dot_general | solution.py:253
  139.6 46.1 %reduce-scatter.2.cloned.1.call-done = bf16[384,512]{1,0:T(8,128)(2,1)} async-done(((bf16[384,4096]{1,0:T(8,128)(2,1)}), bf16[384,512]{1,0:T(8,128)(2,1)}) %reduce-scatter.2.cloned.1.call-update) | async-done | bytes 393232 | tf_op jit(solution)/shard_map/reduce_scatter | solution.py:258
  (110 shorter events, 17.5 us)
Async XLA Ops:
  6.5 122.8 %all-gather.2.cloned.1.call-start = ((), (), s32[]{:S(2)}) async-start(), calls=%async_computation.1 | async-start | bytes 8519680 | tf_op jit(solution)/shard_map/all_gather | solution.py:255
  7.3 178.4 %reduce-scatter.2.cloned.1.call-start = ((), (), s32[]{:S(2)}) async-start(), calls=%async_computation.2 | async-start | bytes 3538944 | tf_op jit(solution)/shard_map/reduce_scatter | solution.py:258
  8.1 11.7 %collective-permute-start.1 = (bf16[3]{0:T(256)(128)(2,1)S(1)}, bf16[3]{0:T(256)(128)(2,1)S(1)}, u32[]{:S(2)}, u32[]{:S(2)}) collective-permute-start(bf16[3]{0:T(256)(128)(2,1)S(1)} %slice.68), channel_id=1, source_target_pairs={{0,8},{8,16},{16,24},{24,32},{32,40},{40,48},{48,56},{56,64},{64,7... | collective-permute-start | bytes 26 | tf_op jit(solution)/shard_map/ppermute | solution.py:18
  13.3 8.0 %collective-permute-start = (bf16[3,1280]{1,0:T(4,128)(2,1)S(1)}, bf16[3,1280]{1,0:T(4,128)(2,1)S(1)}, u32[]{:S(2)}, u32[]{:S(2)}) collective-permute-start(bf16[3,1280]{1,0:T(4,128)(2,1)S(1)} %slice.66), channel_id=1, source_target_pairs={{0,8},{8,16},{16,24},{24,32},{32,40},{40,48},{48,56},{56,64},{64,7... | collective-permute-start | bytes 23048 | tf_op jit(solution)/shard_map/ppermute | solution.py:18
  17.9 4.9 %copy-start.1 = (f32[1280]{0:T(1024)S(1)}, f32[1280]{0:T(1024)}, u32[]{:S(2)}) copy-start(f32[1280]{0:T(1024)} %param.24) | copy-start | bytes 15364
  25.6 8.3 %copy-start = (bf16[384,1,1280]{2,0,1:T(8,128)(2,1)}, bf16[384,1,1280]{2,0,1:T(8,128)(2,1)S(1)}, u32[]{:S(2)}) copy-start(bf16[384,1,1280]{2,0,1:T(8,128)(2,1)S(1)} %fusion.44) | copy-start | bytes 2949124
  113.2 16.2 %copy-start.2 = (f32[1024]{0:T(1024)S(1)}, f32[1024]{0:T(1024)}, u32[]{:S(2)}) copy-start(f32[1024]{0:T(1024)} %param.25) | copy-start | bytes 12292
Sparse Core Ops, SparseCore 0:
  10.7 98.9 all-gather.1
  139.7 45.9 reduce-scatter.1

commit v2 on v1

--- a/solution.py
+++ b/solution.py
@@ -133,6 +133,157 @@
     return entering.reshape(HG, P_SIZE, N).astype(jnp.float32)
 
 
+HEADS = 8
+HALF = 192
+COLS = 256
+
+
+def project_kernel(
+    mine_ref, weight_ref, square_ref, out_ref, other_buf, send_buf, recv_buf, square_buf,
+    own_buf, back_buf, land_buf, a_s, a_r, send_sem, recv_sem, q_s, q_r, b_s, b_r,
+):
+    place = lax.axis_index("seq")
+    h = lax.axis_index("head")
+    core = place % 2
+    partner = place + 1 - 2 * core
+    ways = ((h + 1) % HEADS, (h + HEADS - 1) % HEADS)
+    peers = [(h + k) % HEADS for k in range(1, HEADS)]
+    barrier = pltpu.get_barrier_semaphore()
+    pl.semaphore_signal(barrier, 1, device_id={"seq": partner}, device_id_type=MESH)
+    for peer in peers:
+        pl.semaphore_signal(barrier, 1, device_id={"head": peer}, device_id_type=MESH)
+    pl.semaphore_wait(barrier, HEADS)
+    swap = pltpu.make_async_remote_copy(
+        mine_ref, other_buf, a_s, a_r, device_id={"seq": partner}, device_id_type=MESH
+    )
+    swap.start()
+    tokens = (mine_ref, other_buf)
+
+    def partial(step, way, side):
+        chunk = (h + 2 * HEADS - 1 - step) % HEADS if way == 0 else (h + 1 + step) % HEADS
+        start = pl.multiple_of(chunk * COLS, COLS)
+        return lax.dot_general(
+            tokens[side][way * HALF : (way + 1) * HALF, :],
+            weight_ref[pl.ds(start, COLS), :],
+            (((1,), (1,)), ((), ())),
+            preferred_element_type=jnp.float32,
+        )
+
+    def hop(step, way, side):
+        return pltpu.make_async_remote_copy(
+            send_buf.at[step, way, side], recv_buf.at[step, way, side],
+            send_sem.at[step, way, side], recv_sem.at[step, way, side],
+            device_id={"head": ways[way]}, device_id_type=MESH,
+        )
+
+    def summed(step, way, side):
+        term = partial(step, way, side)
+        hop(step - 1, way, side).wait_recv()
+        return term + recv_buf[step - 1, way, side].astype(jnp.float32)
+
+    for way in range(2):
+        send_buf[0, way, 0] = partial(0, way, 0).astype(jnp.bfloat16)
+        hop(0, way, 0).start()
+    squares = []
+    for k, peer in enumerate(peers):
+        squares.append(
+            pltpu.make_async_remote_copy(
+                square_ref, square_buf.at[h], q_s.at[k], q_r.at[k],
+                device_id={"head": peer}, device_id_type=MESH,
+            )
+        )
+        squares[-1].start()
+    square_buf[h] = square_ref[...]
+    swap.wait()
+    for way in range(2):
+        send_buf[0, way, 1] = partial(0, way, 1).astype(jnp.bfloat16)
+        hop(0, way, 1).start()
+
+    def one(step, carry):
+        for side in range(2):
+            for way in range(2):
+                send_buf[step, way, side] = summed(step, way, side).astype(jnp.bfloat16)
+                hop(step, way, side).start()
+        return carry
+
+    lax.fori_loop(1, HEADS - 1, one, 0)
+    last = HEADS - 1
+    for way in range(2):
+        own_buf[way * HALF : (way + 1) * HALF, :] = summed(last, way, 0)
+    backs = []
+    for way in range(2):
+        rows = pl.ds(way * HALF, HALF)
+        back_buf[way * HALF : (way + 1) * HALF, :] = summed(last, way, 1).astype(jnp.bfloat16)
+        backs.append(
+            pltpu.make_async_remote_copy(
+                back_buf.at[rows], land_buf.at[rows], b_s.at[way], b_r.at[way],
+                device_id={"seq": partner}, device_id_type=MESH,
+            )
+        )
+        backs[-1].start()
+    for copy in squares:
+        copy.wait()
+    total = square_buf[0]
+    for k in range(1, HEADS):
+        total = total + square_buf[k]
+    scale = lax.rsqrt(total / DI + 1e-05)
+    scale = jnp.concatenate([scale] * 16, axis=0).T
+    for copy in backs:
+        copy.wait()
+    for part in range(3):
+        rows = slice(part * 128, (part + 1) * 128)
+        factor = jnp.broadcast_to(scale[:, part : part + 1], (128, 128))
+        own = own_buf[rows, :]
+        other = land_buf[rows, :].astype(jnp.float32)
+        for x in range(4):
+            mine = own[:, x * 64 : (x + 1) * 64]
+            theirs = other[:, x * 64 : (x + 1) * 64]
+            block = jnp.where(
+                core == 0,
+                jnp.concatenate([mine, theirs], axis=1),
+                jnp.concatenate([theirs, mine], axis=1),
+            )
+            out_ref[rows, x * 128 : (x + 1) * 128] = (block * factor).astype(jnp.bfloat16)
+
+    def drain(step, carry):
+        for side in range(2):
+            for way in range(2):
+                hop(step, way, side).wait_send()
+        return carry
+
+    lax.fori_loop(0, HEADS - 1, drain, 0)
+
+
+def project(gained, weight, squares):
+    steps = HEADS - 1
+    return pl.pallas_call(
+        project_kernel,
+        out_shape=jax.ShapeDtypeStruct((2 * HALF, 2 * COLS), jnp.bfloat16),
+        in_specs=[pl.BlockSpec(memory_space=pltpu.VMEM)] * 3,
+        out_specs=pl.BlockSpec(memory_space=pltpu.VMEM),
+        scratch_shapes=[
+            pltpu.VMEM((2 * HALF, 1024), jnp.bfloat16),
+            pltpu.VMEM((steps, 2, 2, HALF, COLS), jnp.bfloat16),
+            pltpu.VMEM((steps, 2, 2, HALF, COLS), jnp.bfloat16),
+            pltpu.VMEM((HEADS, 8, 128), jnp.float32),
+            pltpu.VMEM((2 * HALF, COLS), jnp.float32),
+            pltpu.VMEM((2 * HALF, COLS), jnp.bfloat16),
+            pltpu.VMEM((2 * HALF, COLS), jnp.bfloat16),
+            pltpu.SemaphoreType.DMA,
+            pltpu.SemaphoreType.DMA,
+            pltpu.SemaphoreType.DMA((steps, 2, 2)),
+            pltpu.SemaphoreType.DMA((steps, 2, 2)),
+            pltpu.SemaphoreType.DMA((steps,)),
+            pltpu.SemaphoreType.DMA((steps,)),
+            pltpu.SemaphoreType.DMA((2,)),
+            pltpu.SemaphoreType.DMA((2,)),
+        ],
+        compiler_params=pltpu.CompilerParams(collective_id=1, has_side_effects=True),
+        cost_estimate=pl.CostEstimate(flops=4 * 10**9, bytes_accessed=10**7, transcendentals=0),
+        name="project",
+    )(gained, weight, squares)
+
+
 def block_local(item):
     xc, bc, cc, dtc, lc, sc = item
     cumul = jnp.cumsum(lc, axis=1)
@@ -182,6 +333,8 @@
     starts,
 ):
     tok = xbc.shape[0]
+    cores = [[2 * i + c for i in range(lax.axis_size("seq") // 2)] for c in range(2)]
+    weight = lax.all_gather(out_weight.T, "seq", axis_index_groups=cores, axis=0, tiled=True)
     width = conv_weight.shape[0]
     chans = xbc.shape[1]
     groups = chans // GW
@@ -246,16 +399,10 @@
         jnp.float32
     )
     gated = y_all.reshape(tok, heads * P_SIZE) * jax.nn.silu(gate_z.astype(jnp.float32))
-    total_sq = lax.psum(jnp.sum(gated * gated, axis=1), "head")
-    normed = (gated * lax.rsqrt(total_sq / DI + 1e-05)[:, None] * norm_gain[None, :]).astype(
-        jnp.bfloat16
-    )
-    terms = jnp.dot(
-        normed,
-        lax.all_gather(out_weight, "seq", axis=1, tiled=True),
-        preferred_element_type=jnp.float32,
-    )
-    return lax.psum_scatter(terms.astype(jnp.bfloat16), "head", scatter_dimension=1, tiled=True)
+    squares = jnp.sum(gated * gated, axis=1).reshape(tok // 128, 128)
+    squares = jnp.pad(squares, ((0, 8 - tok // 128), (0, 0)))
+    gained = (gated * norm_gain[None, :]).astype(jnp.bfloat16)
+    return project(gained, weight, squares)
 
 
 def solution(mesh):

time: 196 us -> 166 us (0.85); the launches traced: 192 us -> 165 us
  Pallas kernels: 40.3 us -> 87.4 us
  waiting for transfers between devices: 46.8 us -> 0.98 us
  matrix products: 26 us -> 9.9 us
  blocking collectives: 13.6 us -> 0 us
    pallas_call x0 -> x1, Pallas kernels: none -> 51.2 us  [project(): pl.pallas_call(project_kernel, out_shape=jax.ShapeDtypeStruct((2 * HALF,...]
    reduce_scatter x1 -> x0, waiting for transfers between devices: 46.1 us -> none  [body(): lax.psum_scatter(terms.astype(jnp.bfloat16), 'head', scatter_dimension=1,...]
    psum x1 -> x0, blocking collectives: 13.6 us -> none  [body(): total_sq = lax.psum(jnp.sum(gated * gated, axis=1), 'head')]
    dot_general x1 -> x0, matrix products: 10.2 us -> none  [body(): jnp.dot(normed, lax.all_gather(out_weight, 'seq', axis=1, tiled=True), pr...]
    pallas_call x1, Pallas kernels: 40.3 us -> 36.2 us  [chain_states(): pl.pallas_call(states_kernel, out_shape=jax.ShapeDtypeStruct((ROW, 2, P_S...]
    dot_general x3, matrix products: 7.01 us -> 4.12 us  [block_inner(): jnp.einsum('hts,shp->thp', weights, xc, preferred_element_type=jnp.float32)]
    dot_general x3, matrix products: 4.45 us -> 1.59 us  [block_local(): jnp.einsum('shp,hsn->hpn', xc, scaled, preferred_element_type=jnp.float32)]
    unnamed x6 -> x9, local copies, waits for them, and re-layouts: 0.01 us -> 2.71 us
  transfers between devices with their start and end apart: 4 -> 3, of which waited for: 1 -> 1; matrix products, arithmetic and copies ran while one was open for 31% -> 31% of each run, Pallas kernels for 21% -> 22%
where the time goes in v2:
time: 166 us; the launch traced here: 165 us
  Pallas kernels  87.4 us (53%)
  other arithmetic  22.6 us (14%)
  local copies, waits for them, and re-layouts  21.8 us (13%)
  between operations  13.6 us (8%)
  matrix products  9.9 us (6%)
  starting transfers between devices  6.4 us (4%)
  loops' own time  2.16 us (1%)
    pallas_call x1, Pallas kernels, project(): pl.pallas_call(project_kernel, out_shape=jax.ShapeDtypeStruct((2 * HALF,...  51.2 us
    pallas_call x1, Pallas kernels, chain_states(): pl.pallas_call(states_kernel, out_shape=jax.ShapeDtypeStruct((ROW, 2, P_S...  36.2 us
    ppermute x2, starting transfers between devices, passed_along(): return lax.ppermute(block, axis, route)  6.39 us
    reshape x2, local copies, waits for them, and re-layouts, body(): (y_diag + y_offs).reshape(tok, heads, P_SIZE)  4.13 us
    dot_general x3, matrix products, block_inner(): jnp.einsum('hts,shp->thp', weights, xc, preferred_element_type=jnp.float32)  4.12 us
    dot_general x3, matrix products, apply(): jnp.einsum('thn,hpn->thp', c_heads, state.astype(jnp.bfloat16), preferred...  3.81 us
    add x1, other arithmetic, body(): y_diag + y_offs  3.5 us
  transfers between devices with their start and end apart: 3, of which 1 were waited for; matrix products, arithmetic and copies ran while one was open for 31% of the time, Pallas kernels for 22%

profile of v2, /device:TPU:1, one launch (start us, length us, event | category | flops | bytes accessed | tf_op | source)
XLA Modules:
  0.0 164.9 jit_solution(592903601261219133)
XLA Ops:
  7.3 4.5 %collective-permute-start.1 = (bf16[3]{0:T(256)(128)(2,1)S(1)}, bf16[3]{0:T(256)(128)(2,1)S(1)}, u32[]{:S(2)}, u32[]{:S(2)}) collective-permute-start(bf16[3]{0:T(256)(128)(2,1)S(1)} %slice.68), channel_id=1, source_target_pairs={{0,8},{8,16},{16,24},{24,32},{32,40},{40,48},{48,56},{56,64},{64,7... | collective-permute-start | bytes 26 | tf_op jit(solution)/shard_map/ppermute | solution.py:18
  12.5 1.9 %collective-permute-start = (bf16[3,1280]{1,0:T(4,128)(2,1)S(1)}, bf16[3,1280]{1,0:T(4,128)(2,1)S(1)}, u32[]{:S(2)}, u32[]{:S(2)}) collective-permute-start(bf16[3,1280]{1,0:T(4,128)(2,1)S(1)} %slice.66), channel_id=1, source_target_pairs={{0,8},{8,16},{16,24},{24,32},{32,40},{40,48},{48,56},{56,64},{64,7... | collective-permute-start | bytes 23048 | tf_op jit(solution)/shard_map/ppermute | solution.py:18
  14.5 1.0 reduce-window.22
  15.8 0.9 slice_reduce_fusion.4
  17.4 0.8 compare_select_fusion
  18.3 0.8 mul.216
  20.8 1.4 maximum_convert_fusion
  22.2 1.9 %fusion.44 = bf16[384,1,1280]{2,0,1:T(8,128)(2,1)S(1)} fusion(f32[384]{0:T(512)S(1)} %get-tuple-element.256, f32[387,1280]{1,0:T(8,128)S(1)} %maximum_convert_fusion, f32[1280]{0:T(1024)S(1)} %get-tuple-element.195, f32[384]{0:T(512)S(1)} %get-tuple-element.257, f32[1280]{0:T(1024)S(1)} %get-tuple-element.196, f32[384]{0:T(512)S(1)} %get-tuple-element.255, ...), kind=kLoop, calls=%fused_computation.78 | loop fusion | flops 8355840 | bytes 7894528 | tf_op jit(solution)/shard_map/reshape | solution.py:356
  24.2 0.9 copy-done
  25.1 1.9 %reshape.285 = bf16[3,128,16,64]{3,2,1,0:T(8,128)(2,1)} reshape(bf16[384,1,1024]{2,0,1:T(8,128)(2,1)S(1)} %slice.86) | data formatting | bytes 1572864 | tf_op jit(solution)/shard_map/reshape;reshape | solution.py:364
  27.0 2.0 %copy.21 = bf16[3,128,16,64]{1,3,2,0:T(8,128)(2,1)S(1)} copy(bf16[3,128,16,64]{3,2,1,0:T(8,128)(2,1)} %reshape.285) | data formatting | bytes 1572864 | tf_op jit(solution)/shard_map/while | solution.py:376
  29.0 1.4 broadcast.141.clone
  30.4 17.1 %while.41 = (s32[]{:T(128)}, f32[3,128,16,64]{1,3,2,0:T(8,128)}, f32[3,16,64,128]{3,2,1,0:T(8,128)S(1)}, f32[3,16]{1,0:T(4,128)S(1)}, f32[3,16,128]{2,1,0:T(8,12...) while((s32[]{:T(128)}, f32[3,128,16,64]{1,3,2,0:T(8,128)}, ...), condition=%wide.region_7.8_spmd, body=%wide.region_4.7_spmd.sunk | while | flops 73752848 | bytes 2099019 | solution.py:376
  32.1 1.3 fusion.73
  37.8 1.4 fusion.73
  43.5 1.4 fusion.73
  48.5 0.7 pad_maximum_fusion.mine_ref
  49.3 36.2 %chain_states.1 = bf16[8,2,64,128]{3,2,1,0:T(8,128)(2,1)} custom-call(bf16[8,2,80,128]{3,2,1,0:T(8,128)(2,1)} %pad_maximum_fusion.mine_ref), custom_call_target="tpu_custom_call" | custom-call | flops 10000000 | bytes 1000000 | tf_op jit(solution)/shard_map/chain_states/pallas_call | solution.py:116
  85.5 1.0 bitcast_convert_fusion.1
  86.5 1.4 broadcast.141
  87.9 4.4 %while.42 = (s32[]{:T(128)}, f32[16,64,128]{2,1,0:T(8,128)S(1)}, f32[3,128,16,64]{1,3,2,0:T(8,128)}, f32[3,16]{1,0:T(4,128)S(1)}, f32[3,16,64,128]{3,2,1,0:T(8,1...) while((s32[]{:T(128)}, f32[16,64,128]{2,1,0:T(8,128)S(1)}, ...), condition=%wide.region_11.12_spmd, body=%wide.region_10.11_spmd.sunk | while | flops 34078720 | bytes 2744625 | solution.py:397
  87.9 1.3 fusion.79
  89.3 1.3 fusion.79
  90.8 1.3 fusion.79
  92.3 3.5 %add.70 = f32[3,128,16,64]{1,3,2,0:T(8,128)} add(f32[3,128,16,64]{1,3,2,0:T(8,128)} %get-tuple-element.130, f32[3,128,16,64]{1,3,2,0:T(8,128)} %get-tuple-element.136) | non-fusion elementwise | flops 393216 | bytes 4718592 | tf_op jit(solution)/shard_map/add | solution.py:398
  95.8 2.3 %copy.32 = f32[3,128,16,64]{3,2,1,0:T(8,128)S(1)} copy(f32[3,128,16,64]{1,3,2,0:T(8,128)} %add.70) | data formatting | bytes 3145728 | tf_op jit(solution)/shard_map/reshape | solution.py:398
  98.1 1.8 %reshape.286 = f32[384,1024]{1,0:T(8,128)} reshape(f32[3,128,16,64]{3,2,1,0:T(8,128)S(1)} %copy.32) | data formatting | bytes 3145728 | tf_op jit(solution)/shard_map/reshape | solution.py:398
  99.9 2.6 %multiply_reduce_fusion.1 = (f32[384]{0:T(512)S(1)}, f32[384,1024]{1,0:T(8,128)S(1)}) fusion(bf16[384,1024]{1,0:T(8,128)(2,1)} %param.18, f32[384,1024]{1,0:T(8,128)} %reshape.286, bf16[384,1,1280]{2,0,1:T(8,128)(2,1)} %copy-done, f32[1024]{0:T(1024)S(1)} %mul.217), kind=kLoop, calls=%fused_computation.75 | loop fusion | flops 4324992 | bytes 4724224 | tf_op jit(solution)/shard_map/reduce_sum | solution.py:402
  103.1 1.1 multiply_convert_fusion.5.mine_ref
  104.2 1.0 all-gather.2.cloned.1.call-done.weight_ref
  105.1 51.2 %project.1 = bf16[384,512]{1,0:T(8,128)(2,1)} custom-call(bf16[384,1024]{1,0:T(8,128)(2,1)} %multiply_convert_fusion.5.mine_ref, bf16[2048,1024]{1,0:T(8,128)(2,1)} %all-gather.2.cloned.1.call-done.weight_ref, f32[8,128]{1,0:T(8,128)} %pad.4.square_ref), custom_call_target="tpu_custom_call" | custom-call | flops 4000000000 | bytes 10000000 | tf_op jit(solution)/shard_map/project/pallas_call | solution.py:259
  156.3 1.8 %copy.81 = bf16[384,512]{1,0:T(8,128)(2,1)} copy(bf16[384,512]{1,0:T(8,128)(2,1)} %project.1) | data formatting | bytes 786432
  (110 shorter events, 17.7 us)
Async XLA Ops:
  6.5 98.6 %all-gather.2.cloned.1.call-start = ((), (), s32[]{:S(2)}) async-start(), calls=%async_computation | async-start | bytes 4325376 | tf_op jit(solution)/shard_map/all_gather | solution.py:337
  7.3 11.9 %collective-permute-start.1 = (bf16[3]{0:T(256)(128)(2,1)S(1)}, bf16[3]{0:T(256)(128)(2,1)S(1)}, u32[]{:S(2)}, u32[]{:S(2)}) collective-permute-start(bf16[3]{0:T(256)(128)(2,1)S(1)} %slice.68), channel_id=1, source_target_pairs={{0,8},{8,16},{16,24},{24,32},{32,40},{40,48},{48,56},{56,64},{64,7... | collective-permute-start | bytes 26 | tf_op jit(solution)/shard_map/ppermute | solution.py:18
  12.5 8.2 %collective-permute-start = (bf16[3,1280]{1,0:T(4,128)(2,1)S(1)}, bf16[3,1280]{1,0:T(4,128)(2,1)S(1)}, u32[]{:S(2)}, u32[]{:S(2)}) collective-permute-start(bf16[3,1280]{1,0:T(4,128)(2,1)S(1)} %slice.66), channel_id=1, source_target_pairs={{0,8},{8,16},{16,24},{24,32},{32,40},{40,48},{48,56},{56,64},{64,7... | collective-permute-start | bytes 23048 | tf_op jit(solution)/shard_map/ppermute | solution.py:18
  18.2 3.9 %copy-start.1 = (bf16[384,1280]{1,0:T(8,128)(2,1)S(1)}, bf16[384,1280]{1,0:T(8,128)(2,1)}, u32[]{:S(2)}) copy-start(bf16[384,1280]{1,0:T(8,128)(2,1)} %param.17) | copy-start | bytes 2949124
  18.3 3.9 %copy-start.2 = (f32[1280]{0:T(1024)S(1)}, f32[1280]{0:T(1024)}, u32[]{:S(2)}) copy-start(f32[1280]{0:T(1024)} %param.24) | copy-start | bytes 15364
  24.1 1.0 copy-start
  99.9 3.2 %copy-start.3 = (f32[1024]{0:T(1024)S(1)}, f32[1024]{0:T(1024)}, u32[]{:S(2)}) copy-start(f32[1024]{0:T(1024)} %param.25) | copy-start | bytes 12292
Sparse Core Ops, SparseCore 0:
  14.6 90.4 all-gather.1

commit v3 on v0

v3 whole, which is shorter than its diff:
```python
import jax
import jax.numpy as jnp
from jax import lax
from jax.experimental import pallas as pl
from jax.experimental.pallas import tpu as pltpu
from jax.sharding import PartitionSpec as P

MESH = pl.DeviceIdType.MESH
P_SIZE = 64
N = 128
DI = 8192
HG = 16
GW = 1280
TOK = 384
RIM = 16
WIDTH = HG * P_SIZE
PART = P_SIZE + 16
ROW = 8
HEADS = 8
HALF = 192
COLS = 256
BF = jnp.bfloat16
F32 = jnp.float32
SHAPES = dict(
    halo=((RIM, GW), BF),
    halo_starts=((8, N), F32),
    ext=((RIM + TOK, GW), F32),
    flags=((RIM + TOK, N), F32),
    keep=((3, TOK, N), F32),
    unit=((TOK, GW), BF),
    spread=((N, WIDTH), BF),
    scaled=((TOK, WIDTH), BF),
    linear=((TOK, WIDTH), F32),
    enter=((TOK, N), BF),
    masked_c=((TOK, N), BF),
    mine=((ROW, 2, PART, N), BF),
    row=((ROW, 2, PART, N), BF),
    total=((2, PART, N), BF),
    column=((ROW, 2, PART, N), BF),
    back=((ROW, 2, P_SIZE, N), BF),
    land=((ROW, 2, P_SIZE, N), BF),
    weight=((HEADS, COLS, WIDTH), BF),
    gained=((TOK, WIDTH), BF),
    other=((TOK, WIDTH), BF),
    send=((HEADS - 1, 2, 2, HALF, COLS), BF),
    recv=((HEADS - 1, 2, 2, HALF, COLS), BF),
    square=((8, N), F32),
    squares=((HEADS, 8, N), F32),
    own=((TOK, COLS), F32),
    home=((TOK, COLS), BF),
    home_land=((TOK, COLS), BF),
)
SEMS = dict(
    halo=(2,), wx=(3,), wz=(4, 2), rows=(7,), columns=(7,), backs=(7,),
    swap=(1,), ring=(HEADS - 1, 2, 2), square=(7,), home=(2,),
)


def dot(a, b, ca=1, cb=0):
    return lax.dot_general(a, b, (((ca,), (cb,)), ((), ())), preferred_element_type=F32)


def iota(shape, axis):
    return lax.broadcasted_iota(jnp.int32, shape, axis)


def split_lanes(value, axis):
    high = value.astype(BF).astype(F32)
    index = iota(value.shape, axis)
    pair = jnp.where(index < HG, high, jnp.where(index < 2 * HG, value - high, 0.0))
    return pair.astype(BF)


def decay_of(tile):
    both = tile.astype(F32)
    return both[0:1] + both[8:9]


def decay_rows(decay):
    high = decay.astype(BF).astype(F32)
    return jnp.concatenate([high, decay - high], axis=0).astype(BF)


def columns_of(rows):
    return jnp.concatenate([rows] * (N // rows.shape[0]), axis=0).T


def layer_kernel(
    xbc_ref, gate_ref, dt_ref, bias_ref, log_ref, skip_ref, taps_ref, shift_ref, gain_ref,
    weight_ref, starts_ref, out_ref, *scratch,
):
    names = list(SHAPES)
    b = dict(zip(names, scratch[: len(names)]))
    sems = scratch[len(names) :]
    ss = dict(zip(SEMS, sems[: len(SEMS)]))
    rs = dict(zip(SEMS, sems[len(SEMS) :]))
    place = lax.axis_index("seq")
    h = lax.axis_index("head")
    z = place // ROW
    j = place % ROW
    x = j // 2
    core = j % 2
    partner = place + 1 - 2 * core
    after = (place + 1) % 64
    before = (place + 63) % 64
    row_peers = [z * ROW + (j + k) % ROW for k in range(1, ROW)]
    column_peers = [((z + k) % ROW) * ROW + j for k in range(1, ROW)]
    head_peers = [(h + k) % HEADS for k in range(1, HEADS)]
    ways = (head_peers[0], head_peers[-1])

    barrier = pltpu.get_barrier_semaphore()
    for peer in row_peers + column_peers + [after, before]:
        pl.semaphore_signal(barrier, 1, device_id={"seq": peer}, device_id_type=MESH)
    for peer in head_peers:
        pl.semaphore_signal(barrier, 1, device_id={"head": peer}, device_id_type=MESH)
    pl.semaphore_wait(barrier, 23)

    def copy(src, dst, name, at, axis, peer):
        return pltpu.make_async_remote_copy(
            src, dst, ss[name].at[at], rs[name].at[at],
            device_id={axis: peer}, device_id_type=MESH,
        )

    halo = [
        copy(xbc_ref.at[pl.ds(TOK - RIM, RIM)], b["halo"], "halo", 0, "seq", after),
        copy(starts_ref.at[:, pl.ds(TOK - N, N)], b["halo_starts"], "halo", 1, "seq", after),
    ]
    for one in halo:
        one.start()
    block = pl.ds(pl.multiple_of(x * 64, 64), 64)
    around = []
    for k in range(1, 4):
        peer = z * ROW + ((x + k) % 4) * 2 + core
        around.append(copy(weight_ref, b["weight"].at[z, block], "wx", k - 1, "seq", peer))
        around[-1].start()
    b["weight"][z, block] = weight_ref[...]

    def pass_on(step):
        up = (z + 9 - step) % ROW
        down = (z + step - 1) % ROW
        rows = (pl.ds(0, COLS), pl.ds(0, COLS))
        if step == 4:
            rows = (pl.ds(0, COLS // 2), pl.ds(COLS // 2, COLS // 2))
        pair = []
        for way, (chunk, peer) in enumerate(((up, column_peers[0]), (down, column_peers[-1]))):
            part = b["weight"].at[chunk, rows[way]]
            pair.append(copy(part, part, "wz", (step - 1, way), "seq", peer))
            pair[-1].start()
        return pair

    starts = starts_ref[...]
    lower = iota((TOK, TOK), 0) >= iota((TOK, TOK), 1)
    tri = jnp.where(lower, 1.0, 0.0).astype(BF)
    flag_col = columns_of(starts)
    dt_row = dt_ref[...].astype(F32) + jnp.concatenate([bias_ref[...]] * 3, axis=1)
    dt_row = jnp.maximum(dt_row, 0.0) + jnp.log1p(jnp.exp(-jnp.abs(dt_row)))
    dt_col = columns_of(dt_row)
    log_col = columns_of(-jnp.exp(jnp.concatenate([log_ref[...]] * 3, axis=1)) * dt_row)
    log_high = log_col.astype(BF)
    log_low = (log_col - log_high.astype(F32)).astype(BF)
    cumul = dot(tri, log_high) + dot(tri, log_low)
    runs = dot(tri, flag_col.astype(BF))
    runs_row = dot(starts.astype(BF), tri, 1, 1)
    growth = jnp.exp(cumul)
    b["enter"][...] = split_lanes(growth, 1)
    inverse = split_lanes(jnp.exp(-cumul) * dt_col, 1)
    low_index = iota((N, WIDTH), 0)
    spread = (low_index < 2 * HG) & ((low_index & (HG - 1)) == (iota((N, WIDTH), 1) >> 6))
    b["spread"][...] = jnp.where(spread, 1.0, 0.0).astype(BF)

    for one in halo:
        one.wait()
    real = jnp.where(place > 0, 1.0, 0.0)
    b["ext"][:RIM] = b["halo"][...].astype(F32) * real
    b["ext"][RIM:] = xbc_ref[...].astype(F32)
    b["flags"][:RIM] = columns_of(b["halo_starts"][...])[N - RIM :] * real
    b["flags"][RIM:] = flag_col
    crossed = b["flags"][RIM:]
    for lag in range(1, 4):
        b["keep"][lag - 1] = jnp.where(crossed == 0.0, 1.0, 0.0)
        crossed = crossed + b["flags"][RIM - lag : RIM - lag + TOK]

    def conv(c, carry):
        lanes = pl.ds(pl.multiple_of(c * N, N), N)
        acc = shift_ref[:, lanes] + taps_ref[3:4, lanes] * b["ext"][RIM:, lanes]
        for lag in range(1, 4):
            early = b["ext"][pl.ds(RIM - lag, TOK), lanes]
            acc = acc + taps_ref[3 - lag : 4 - lag, lanes] * early * b["keep"][lag - 1]
        b["unit"][:, lanes] = (acc / (1.0 + jnp.exp(-acc))).astype(BF)
        return carry

    lax.fori_loop(0, GW // N, conv, 0)
    for one in around:
        one.wait()
    moved = [pass_on(1)]

    for c in range(WIDTH // N):
        lanes = slice(c * N, (c + 1) * N)
        factor = dot(inverse, b["spread"][:, lanes])
        b["scaled"][:, lanes] = (b["unit"][:, lanes].astype(F32) * factor).astype(BF)
    bmat = b["unit"][:, WIDTH : WIDTH + N]
    cmat = b["unit"][:, WIDTH + N :]
    last = runs[TOK - 1 : TOK, :]
    tail_b = jnp.where(runs == last, bmat.astype(F32), 0.0).astype(BF)
    state = dot(b["scaled"][...], tail_b, 0, 0)
    ends = jnp.broadcast_to(growth[TOK - 1 : TOK, :], (N, N)).T
    ends = dot(b["spread"][...], split_lanes(ends, 0), 0, 0)
    state = state * ends
    unbroken = jnp.where(last == 0.0, 1.0, 0.0)
    for head in range(HG):
        at = head * P_SIZE
        b["mine"][head // 2, head % 2, :P_SIZE] = state[at : at + P_SIZE].astype(BF)
        b["mine"][head // 2, head % 2, P_SIZE:] = decay_rows(ends[at : at + 8] * unbroken)
    copies = []
    for k in range(1, ROW):
        to = (j + k) % ROW
        copies.append(copy(b["mine"].at[to], b["row"].at[j], "rows", k - 1, "seq", row_peers[k - 1]))
        copies[-1].start()
    b["row"][j] = b["mine"][j]
    scores = dot(cmat, bmat, 1, 1)
    same = lower & (jnp.concatenate([runs] * 3, axis=1) == runs_row[0:1])
    scores = jnp.where(same, scores, 0.0).astype(BF)
    b["masked_c"][...] = jnp.where(runs == 0.0, cmat.astype(F32), 0.0).astype(BF)
    for c in range(4):
        lanes = slice(c * COLS, (c + 1) * COLS)
        b["linear"][:, lanes] = dot(scores, b["scaled"][:, lanes])
    for one in copies:
        one.wait()

    for head in range(2):
        total = b["row"][0, head, :P_SIZE].astype(F32)
        decay = decay_of(b["row"][0, head, P_SIZE:])
        for i in range(1, ROW):
            one = decay_of(b["row"][i, head, P_SIZE:])
            total = total * one + b["row"][i, head, :P_SIZE].astype(F32)
            decay = decay * one
        b["total"][head, :P_SIZE] = total.astype(BF)
        b["total"][head, P_SIZE:] = decay_rows(jnp.broadcast_to(decay, (8, N)))
    copies = []
    for k, peer in enumerate(column_peers):
        copies.append(copy(b["total"], b["column"].at[z], "columns", k, "seq", peer))
        copies[-1].start()
    b["column"][z] = b["total"][...]
    for step in (2,):
        for one in moved[-1]:
            one.wait_recv()
        moved.append(pass_on(step))
    for one in copies:
        one.wait()
    for head in range(2):
        state = jnp.zeros((P_SIZE, N), F32)
        for i in range(ROW - 1):
            one = decay_of(b["column"][i, head, P_SIZE:])
            later = state * one + b["column"][i, head, :P_SIZE].astype(F32)
            state = jnp.where(i < z, later, state)
        for i in range(ROW):
            b["back"][i, head] = state.astype(BF)
            if i < ROW - 1:
                one = decay_of(b["row"][i, head, P_SIZE:])
                state = state * one + b["row"][i, head, :P_SIZE].astype(F32)
    copies = []
    for k in range(1, ROW):
        to = (j + k) % ROW
        copies.append(copy(b["back"].at[to], b["land"].at[j], "backs", k - 1, "seq", row_peers[k - 1]))
        copies[-1].start()
    b["land"][j] = b["back"][j]
    for one in moved[-1]:
        one.wait_recv()
    moved.append(pass_on(3))
    for one in copies:
        one.wait()

    square = jnp.zeros((TOK, N), F32)
    for c in range(WIDTH // N):
        lanes = slice(c * N, (c + 1) * N)
        state = b["land"][c].reshape(N, N)
        y = b["linear"][:, lanes] + dot(b["masked_c"][...], state, 1, 1)
        y = y * dot(b["enter"][...], b["spread"][:, lanes])
        y = y + skip_ref[:, lanes] * b["unit"][:, lanes].astype(F32)
        gate = gate_ref[:, lanes].astype(F32)
        gated = y * (gate / (1.0 + jnp.exp(-gate)))
        square = square + gated * gated
        b["gained"][:, lanes] = (gated * gain_ref[:, lanes]).astype(BF)
    square = jnp.sum(square.T, axis=0, keepdims=True)
    b["square"][...] = jnp.concatenate(
        [square[:, i * N : (i + 1) * N] for i in range(3)] + [jnp.zeros((5, N), F32)], axis=0
    )

    swap = copy(b["gained"], b["other"], "swap", 0, "seq", partner)
    swap.start()
    for one in moved[-1]:
        one.wait_recv()
    moved.append(pass_on(4))
    squares = []
    for k, peer in enumerate(head_peers):
        squares.append(copy(b["square"], b["squares"].at[h], "square", k, "head", peer))
        squares[-1].start()
    b["squares"][h] = b["square"][...]
    for one in moved[-1]:
        one.wait_recv()
    tokens = (b["gained"], b["other"])

    def partial(step, way, side):
        chunk = (h + 2 * HEADS - 1 - step) % HEADS if way == 0 else (h + 1 + step) % HEADS
        return dot(tokens[side][way * HALF : (way + 1) * HALF, :], b["weight"][chunk], 1, 1)

    def hop(step, way, side):
        at = (step, way, side)
        return copy(b["send"].at[at], b["recv"].at[at], "ring", at, "head", ways[way])

    def summed(step, way, side):
        term = partial(step, way, side)
        hop(step - 1, way, side).wait_recv()
        return term + b["recv"][step - 1, way, side].astype(F32)

    for side in range(2):
        if side == 1:
            swap.wait()
        for way in range(2):
            b["send"][0, way, side] = partial(0, way, side).astype(BF)
            hop(0, way, side).start()

    def one_step(step, carry):
        for side in range(2):
            for way in range(2):
                b["send"][step, way, side] = summed(step, way, side).astype(BF)
                hop(step, way, side).start()
        return carry

    lax.fori_loop(1, HEADS - 1, one_step, 0)
    final = HEADS - 1
    for way in range(2):
        b["own"][way * HALF : (way + 1) * HALF, :] = summed(final, way, 0)
    homes = []
    for way in range(2):
        rows = pl.ds(way * HALF, HALF)
        b["home"][way * HALF : (way + 1) * HALF, :] = summed(final, way, 1).astype(BF)
        homes.append(
            copy(b["home"].at[rows], b["home_land"].at[rows], "home", way, "seq", partner)
        )
        homes[-1].start()
    for one in squares:
        one.wait()
    total = b["squares"][0]
    for k in range(1, HEADS):
        total = total + b["squares"][k]
    scale = columns_of(lax.rsqrt(total / DI + 1e-05))
    for one in homes:
        one.wait()
    for part in range(3):
        rows = slice(part * N, (part + 1) * N)
        factor = jnp.broadcast_to(scale[:, part : part + 1], (N, N))
        own = b["own"][rows, :]
        other = b["home_land"][rows, :].astype(F32)
        for i in range(4):
            mine = own[:, i * 64 : (i + 1) * 64]
            theirs = other[:, i * 64 : (i + 1) * 64]
            block = jnp.where(
                core == 0,
                jnp.concatenate([mine, theirs], axis=1),
                jnp.concatenate([theirs, mine], axis=1),
            )
            out_ref[rows, i * N : (i + 1) * N] = (block * factor).astype(BF)

    def drain(step, carry):
        for side in range(2):
            for way in range(2):
                hop(step, way, side).wait_send()
        return carry

    lax.fori_loop(0, HEADS - 1, drain, 0)
    for pair in moved:
        for one in pair:
            one.wait_send()


def body(
    xbc,
    gate_z,
    dt_raw,
    dt_bias,
    a_log,
    skip_d,
    conv_weight,
    conv_bias,
    norm_gain,
    out_weight,
    starts,
):
    flags = jnp.broadcast_to(starts.astype(F32)[None, :], (8, TOK))
    bias = jnp.broadcast_to(dt_bias[:, None], (HG, N))
    logs = jnp.broadcast_to(a_log[:, None], (HG, N))
    skip = jnp.broadcast_to(skip_d[:, None], (HG, P_SIZE)).reshape(1, WIDTH)
    sems = [pltpu.SemaphoreType.DMA(shape) for shape in SEMS.values()]
    return pl.pallas_call(
        layer_kernel,
        out_shape=jax.ShapeDtypeStruct((TOK, 2 * COLS), BF),
        in_specs=[pl.BlockSpec(memory_space=pltpu.VMEM)] * 11,
        out_specs=pl.BlockSpec(memory_space=pltpu.VMEM),
        scratch_shapes=[pltpu.VMEM(*spec) for spec in SHAPES.values()] + sems + sems,
        compiler_params=pltpu.CompilerParams(collective_id=0, has_side_effects=True),
        name="layer",
    )(
        xbc, gate_z, dt_raw, bias, logs, skip, conv_weight, conv_bias[None, :],
        norm_gain[None, :], out_weight.T, flags,
    )


def solution(mesh):
    placed = (
        P("seq", "head"),
        P("seq", "head"),
        P("head", "seq"),
        P("head"),
        P("head"),
        P("head"),
        P(None, "head"),
        P("head"),
        P("head"),
        P("head", "seq"),
        P("seq"),
    )
    return jax.shard_map(
        body, mesh=mesh, in_specs=placed, out_specs=P("seq", "head"), check_vma=False
    )
```

time: 372 us -> 124 us (0.33); the launches traced: 366 us -> 123 us
  blocking collectives: 145 us -> 0 us
  waiting for transfers between devices: 136 us -> 0 us
  Pallas kernels: 0 us -> 117 us
  other arithmetic: 21.2 us -> 0.01 us
  matrix products: 20.1 us -> 0 us
  local copies, waits for them, and re-layouts: 20.7 us -> 6.43 us
  between operations: 14 us -> 0.02 us
  starting transfers between devices: 6.48 us -> 0 us
    unnamed x1 -> x0, blocking collectives: 132 us -> none
    pallas_call x0 -> x1, Pallas kernels: none -> 117 us  [body(): pl.pallas_call(layer_kernel, out_shape=jax.ShapeDtypeStruct((TOK, 2 * COL...]
    all_gather x2 -> x0, waiting for transfers between devices: 76.5 us -> none  [the longest x1 58.5 us: body(): lax.all_gather(out_weight, 'seq', axis=1, tiled=True)]
    reduce_scatter x1 -> x0, waiting for transfers between devices: 59 us -> none  [body(): lax.psum_scatter(terms.astype(jnp.bfloat16), 'head', scatter_dimension=1,...]
    dot_general x13 -> x0, matrix products: 20.1 us -> none  [the longest x1 10.2 us: body(): jnp.dot(normed, lax.all_gather(out_weight, 'seq', axis=1, tiled=True), pr...]
    psum x1 -> x0, blocking collectives: 13.3 us -> none  [body(): total_sq = lax.psum(jnp.sum(gated * gated, axis=1), 'head')]
    ppermute x2 -> x0, starting transfers between devices: 6.39 us -> none  [passed_along(): return lax.ppermute(block, axis, route)]
    reshape x10 -> x1, local copies, waits for them, and re-layouts: 6.55 us -> 0.67 us  [body(): skip = jnp.broadcast_to(skip_d[:, None], (HG, P_SIZE)).reshape(1, WIDTH)]
  transfers between devices with their start and end apart: 5 -> 0, of which waited for: 3 -> 0; matrix products, arithmetic and copies ran while one was open for 7% -> 0% of each run, Pallas kernels for 0% -> 0%
where the time goes in v3:
time: 124 us; the launch traced here: 123 us
  Pallas kernels  117 us (94%)
  local copies, waits for them, and re-layouts  6.43 us (5%)
    pallas_call x1, Pallas kernels, body(): pl.pallas_call(layer_kernel, out_shape=jax.ShapeDtypeStruct((TOK, 2 * COL...  117 us

profile of v3, /device:TPU:1, one launch (start us, length us, event | category | flops | bytes accessed | tf_op | source)
XLA Modules:
  0.0 123.4 jit_solution(5738196085987086769)
XLA Ops:
  0.0 0.0 copy-start
  0.0 0.7 copy-done
  0.7 0.0 copy-start.1
  0.7 1.3 %broadcast_in_dim.15.shift_ref = f32[1,1280]{1,0:T(1,128)} reshape(f32[1280]{0:T(1024)} %param.18) | data formatting | bytes 10240 | tf_op jit(solution)/shard_map/broadcast_in_dim | solution.py:404
  2.0 0.0 copy-done.1
  2.0 0.0 copy-start.2
  2.0 0.7 broadcast_in_dim.12.bias_ref
  2.7 0.0 copy-done.2
  2.7 0.0 copy-start.3
  2.7 0.7 broadcast_in_dim.13.log_ref
  3.3 0.0 copy-done.3
  3.3 0.1 broadcast_in_dim.14
  3.4 0.7 reshape.7.skip_ref
  4.1 0.6 broadcast_in_dim.17.starts_ref
  4.7 116.9 %layer.1 = bf16[384,512]{1,0:T(8,128)(2,1)} custom-call(bf16[384,1280]{1,0:T(8,128)(2,1)} %xbc_ref.1, bf16[384,1024]{1,0:T(8,128)(2,1)} %gate_ref.1, bf16[16,384]{1,0:T(8,128)(2,1)} %dt_ref.1, f32[16,128]{1,0:T(8,128)} %broadcast_in_dim.12.bias_ref, f32[16,128]{1,0:T(8,128)} %broadcast_in_dim.13.log_ref, f32[1,1024]{1,0:T(1,128)} %reshape.7.skip_ref, ...), custom_call_target="tpu_custom_call" | custom-call | tf_op jit(solution)/shard_map/layer/pallas_call | solution.py:395
  121.6 1.8 %copy.13 = bf16[384,512]{1,0:T(8,128)(2,1)} copy(bf16[384,512]{1,0:T(8,128)(2,1)} %layer.1) | data formatting | bytes 786432
  (1 shorter events, 0.0 us)
Async XLA Ops:
  0.0 0.7 copy-start
  0.7 1.3 %copy-start.1 = (f32[16]{0:T(128)S(1)}, f32[16]{0:T(128)}, u32[]{:S(2)}) copy-start(f32[16]{0:T(128)} %param.14) | copy-start | bytes 196
  2.0 0.7 copy-start.2
  2.7 0.7 copy-start.3

commit v4 on v3

--- a/solution.py
+++ b/solution.py
@@ -18,12 +18,15 @@
 ROW = 8
 HEADS = 8
 HALF = 192
+PIECE = 96
 COLS = 256
 BF = jnp.bfloat16
 F32 = jnp.float32
 SHAPES = dict(
     halo=((RIM, GW), BF),
     halo_starts=((8, N), F32),
+    starts=((8, TOK), F32),
+    skip=((8, WIDTH), F32),
     ext=((RIM + TOK, GW), F32),
     flags=((RIM + TOK, N), F32),
     keep=((3, TOK, N), F32),
@@ -39,11 +42,13 @@
     column=((ROW, 2, PART, N), BF),
     back=((ROW, 2, P_SIZE, N), BF),
     land=((ROW, 2, P_SIZE, N), BF),
-    weight=((HEADS, COLS, WIDTH), BF),
+    weight_a=((HEADS, COLS, WIDTH // 2), BF),
+    weight_b=((HEADS, COLS, WIDTH // 2), BF),
     gained=((TOK, WIDTH), BF),
     other=((TOK, WIDTH), BF),
-    send=((HEADS - 1, 2, 2, HALF, COLS), BF),
-    recv=((HEADS - 1, 2, 2, HALF, COLS), BF),
+    send=((HEADS - 1, 2, 2, 2, PIECE, COLS), BF),
+    recv=((HEADS - 1, 2, 2, 2, PIECE, COLS), BF),
+    terms=((2, 2, HALF, COLS), F32),
     square=((8, N), F32),
     squares=((HEADS, 8, N), F32),
     own=((TOK, COLS), F32),
@@ -51,8 +56,8 @@
     home_land=((TOK, COLS), BF),
 )
 SEMS = dict(
-    halo=(2,), wx=(3,), wz=(4, 2), rows=(7,), columns=(7,), backs=(7,),
-    swap=(1,), ring=(HEADS - 1, 2, 2), square=(7,), home=(2,),
+    halo=(2,), ax=(3,), az=(4, 2), bz=(4, 2), bx=(ROW, 3), rows=(7,), columns=(7,), backs=(7,),
+    swap=(1,), ring=(HEADS - 1, 2, 2, 2), square=(7,), home=(4,),
 )
 
 
@@ -79,6 +84,15 @@
 def decay_rows(decay):
     high = decay.astype(BF).astype(F32)
     return jnp.concatenate([high, decay - high], axis=0).astype(BF)
+
+
+def two_terms(value):
+    high = value.astype(BF).astype(F32)
+    return high + (value - high).astype(BF).astype(F32)
+
+
+def across(ref):
+    return jnp.concatenate([ref[...]] * (N // HG), axis=1)
 
 
 def columns_of(rows):
@@ -113,7 +127,6 @@
         pl.semaphore_signal(barrier, 1, device_id={"seq": peer}, device_id_type=MESH)
     for peer in head_peers:
         pl.semaphore_signal(barrier, 1, device_id={"head": peer}, device_id_type=MESH)
-    pl.semaphore_wait(barrier, 23)
 
     def copy(src, dst, name, at, axis, peer):
         return pltpu.make_async_remote_copy(
@@ -121,41 +134,66 @@
             device_id={axis: peer}, device_id_type=MESH,
         )
 
+    block = pl.ds(pl.multiple_of(x * 64, 64), 64)
+    halves = (pl.ds(0, WIDTH // 2), pl.ds(WIDTH // 2, WIDTH // 2))
+    side_peers = [z * ROW + ((x + k) % 4) * 2 + core for k in range(1, 4)]
+    sideways = []
+
+    def fan(turn):
+        chunk = (z + turn) % ROW
+        part = b["weight_b"].at[chunk, block]
+        source = weight_ref.at[:, halves[1]] if turn == 0 else part
+        for k, peer in enumerate(side_peers):
+            sideways.append(copy(source, part, "bx", (turn, k), "seq", peer))
+            sideways[-1].start()
+
+    def pass_on(name, step):
+        pair = []
+        for way, peer in enumerate((column_peers[0], column_peers[-1])):
+            chunk = (z + 9 - step) % ROW if way == 0 else (z + step - 1) % ROW
+            first, count = (0, COLS) if name == "az" else (x * 64, 64)
+            if step == 4:
+                count = count // 2
+                first = first + way * count
+            rows = pl.ds(pl.multiple_of(first, count), count)
+            part = b["weight_a" if name == "az" else "weight_b"].at[chunk, rows]
+            source = part
+            if name == "bz" and step == 1:
+                source = weight_ref.at[:, halves[1]]
+            pair.append(copy(source, part, name, (step - 1, way), "seq", peer))
+            pair[-1].start()
+        return pair
+
+    def arrived(pair):
+        for one in pair:
+            one.wait_recv()
+
+    starts = jnp.broadcast_to(starts_ref[...].astype(F32)[None, :], (8, TOK))
+    b["starts"][...] = starts
+    lower = iota((TOK, TOK), 0) >= iota((TOK, TOK), 1)
+    tri = jnp.where(lower, 1.0, 0.0).astype(BF)
+    flag_col = columns_of(starts)
+    pl.semaphore_wait(barrier, 23)
     halo = [
         copy(xbc_ref.at[pl.ds(TOK - RIM, RIM)], b["halo"], "halo", 0, "seq", after),
-        copy(starts_ref.at[:, pl.ds(TOK - N, N)], b["halo_starts"], "halo", 1, "seq", after),
+        copy(
+            b["starts"].at[:, pl.ds(TOK - N, N)], b["halo_starts"], "halo", 1, "seq", after
+        ),
     ]
     for one in halo:
         one.start()
-    block = pl.ds(pl.multiple_of(x * 64, 64), 64)
     around = []
-    for k in range(1, 4):
-        peer = z * ROW + ((x + k) % 4) * 2 + core
-        around.append(copy(weight_ref, b["weight"].at[z, block], "wx", k - 1, "seq", peer))
+    for k, peer in enumerate(side_peers):
+        part = b["weight_a"].at[z, block]
+        around.append(copy(weight_ref.at[:, halves[0]], part, "ax", k, "seq", peer))
         around[-1].start()
-    b["weight"][z, block] = weight_ref[...]
-
-    def pass_on(step):
-        up = (z + 9 - step) % ROW
-        down = (z + step - 1) % ROW
-        rows = (pl.ds(0, COLS), pl.ds(0, COLS))
-        if step == 4:
-            rows = (pl.ds(0, COLS // 2), pl.ds(COLS // 2, COLS // 2))
-        pair = []
-        for way, (chunk, peer) in enumerate(((up, column_peers[0]), (down, column_peers[-1]))):
-            part = b["weight"].at[chunk, rows[way]]
-            pair.append(copy(part, part, "wz", (step - 1, way), "seq", peer))
-            pair[-1].start()
-        return pair
-
-    starts = starts_ref[...]
-    lower = iota((TOK, TOK), 0) >= iota((TOK, TOK), 1)
-    tri = jnp.where(lower, 1.0, 0.0).astype(BF)
-    flag_col = columns_of(starts)
-    dt_row = dt_ref[...].astype(F32) + jnp.concatenate([bias_ref[...]] * 3, axis=1)
-    dt_row = jnp.maximum(dt_row, 0.0) + jnp.log1p(jnp.exp(-jnp.abs(dt_row)))
-    dt_col = columns_of(dt_row)
-    log_col = columns_of(-jnp.exp(jnp.concatenate([log_ref[...]] * 3, axis=1)) * dt_row)
+    low = [pass_on("bz", 1)]
+    fan(0)
+    b["weight_a"][z, block] = weight_ref[:, : WIDTH // 2]
+    b["weight_b"][z, block] = weight_ref[:, WIDTH // 2 :]
+    dt_col = columns_of(dt_ref[...].astype(F32)) + across(bias_ref)
+    dt_col = jnp.maximum(dt_col, 0.0) + jnp.log1p(jnp.exp(-jnp.abs(dt_col)))
+    log_col = -jnp.exp(across(log_ref)) * dt_col
     log_high = log_col.astype(BF)
     log_low = (log_col - log_high.astype(F32)).astype(BF)
     cumul = dot(tri, log_high) + dot(tri, log_low)
@@ -167,7 +205,15 @@
     low_index = iota((N, WIDTH), 0)
     spread = (low_index < 2 * HG) & ((low_index & (HG - 1)) == (iota((N, WIDTH), 1) >> 6))
     b["spread"][...] = jnp.where(spread, 1.0, 0.0).astype(BF)
-
+    skip = jnp.broadcast_to(across(skip_ref), (8, N))
+    skip_high = split_lanes(skip, 1)
+    skip_low = jnp.where(iota((8, N), 1) < HG, skip - two_terms(skip), 0.0).astype(BF)
+    b["skip"][...] = dot(skip_high, b["spread"][...]) + dot(skip_low, b["spread"][...])
+
+    arrived(low[0])
+    low.append(pass_on("bz", 2))
+    fan(1)
+    fan(7)
     for one in halo:
         one.wait()
     real = jnp.where(place > 0, 1.0, 0.0)
@@ -182,7 +228,7 @@
 
     def conv(c, carry):
         lanes = pl.ds(pl.multiple_of(c * N, N), N)
-        acc = shift_ref[:, lanes] + taps_ref[3:4, lanes] * b["ext"][RIM:, lanes]
+        acc = shift_ref[lanes][None, :] + taps_ref[3:4, lanes] * b["ext"][RIM:, lanes]
         for lag in range(1, 4):
             early = b["ext"][pl.ds(RIM - lag, TOK), lanes]
             acc = acc + taps_ref[3 - lag : 4 - lag, lanes] * early * b["keep"][lag - 1]
@@ -192,7 +238,7 @@
     lax.fori_loop(0, GW // N, conv, 0)
     for one in around:
         one.wait()
-    moved = [pass_on(1)]
+    high = [pass_on("az", 1)]
 
     for c in range(WIDTH // N):
         lanes = slice(c * N, (c + 1) * N)
@@ -224,6 +270,8 @@
     for c in range(4):
         lanes = slice(c * COLS, (c + 1) * COLS)
         b["linear"][:, lanes] = dot(scores, b["scaled"][:, lanes])
+    arrived(low[1])
+    low.append(pass_on("bz", 3))
     for one in copies:
         one.wait()
 
@@ -241,10 +289,14 @@
         copies.append(copy(b["total"], b["column"].at[z], "columns", k, "seq", peer))
         copies[-1].start()
     b["column"][z] = b["total"][...]
-    for step in (2,):
-        for one in moved[-1]:
-            one.wait_recv()
-        moved.append(pass_on(step))
+    fan(2)
+    fan(6)
+    arrived(low[2])
+    low.append(pass_on("bz", 4))
+    fan(3)
+    fan(5)
+    arrived(high[0])
+    high.append(pass_on("az", 2))
     for one in copies:
         one.wait()
     for head in range(2):
@@ -264,19 +316,22 @@
         copies.append(copy(b["back"].at[to], b["land"].at[j], "backs", k - 1, "seq", row_peers[k - 1]))
         copies[-1].start()
     b["land"][j] = b["back"][j]
-    for one in moved[-1]:
-        one.wait_recv()
-    moved.append(pass_on(3))
+    arrived(low[3])
+    fan(4)
+    arrived(high[1])
+    high.append(pass_on("az", 3))
     for one in copies:
         one.wait()
 
+    arrived(high[2])
+    high.append(pass_on("az", 4))
     square = jnp.zeros((TOK, N), F32)
     for c in range(WIDTH // N):
         lanes = slice(c * N, (c + 1) * N)
         state = b["land"][c].reshape(N, N)
         y = b["linear"][:, lanes] + dot(b["masked_c"][...], state, 1, 1)
         y = y * dot(b["enter"][...], b["spread"][:, lanes])
-        y = y + skip_ref[:, lanes] * b["unit"][:, lanes].astype(F32)
+        y = y + b["skip"][0:1, lanes] * b["unit"][:, lanes].astype(F32)
         gate = gate_ref[:, lanes].astype(F32)
         gated = y * (gate / (1.0 + jnp.exp(-gate)))
         square = square + gated * gated
@@ -288,56 +343,66 @@
 
     swap = copy(b["gained"], b["other"], "swap", 0, "seq", partner)
     swap.start()
-    for one in moved[-1]:
-        one.wait_recv()
-    moved.append(pass_on(4))
     squares = []
     for k, peer in enumerate(head_peers):
         squares.append(copy(b["square"], b["squares"].at[h], "square", k, "head", peer))
         squares[-1].start()
     b["squares"][h] = b["square"][...]
-    for one in moved[-1]:
-        one.wait_recv()
+    arrived(high[3])
+    arrived(sideways)
     tokens = (b["gained"], b["other"])
 
-    def partial(step, way, side):
-        chunk = (h + 2 * HEADS - 1 - step) % HEADS if way == 0 else (h + 1 + step) % HEADS
-        return dot(tokens[side][way * HALF : (way + 1) * HALF, :], b["weight"][chunk], 1, 1)
-
-    def hop(step, way, side):
-        at = (step, way, side)
+    def prepare(step, side):
+        for way in range(2):
+            chunk = (h + 2 * HEADS - 1 - step) % HEADS if way == 0 else (h + 1 + step) % HEADS
+            rows = slice(way * HALF, (way + 1) * HALF)
+            term = dot(tokens[side][rows, : WIDTH // 2], b["weight_a"][chunk], 1, 1)
+            term = term + dot(tokens[side][rows, WIDTH // 2 :], b["weight_b"][chunk], 1, 1)
+            b["terms"][way, side] = term
+
+    def hop(step, way, side, piece):
+        at = (step, way, side, piece)
         return copy(b["send"].at[at], b["recv"].at[at], "ring", at, "head", ways[way])
 
-    def summed(step, way, side):
-        term = partial(step, way, side)
-        hop(step - 1, way, side).wait_recv()
-        return term + b["recv"][step - 1, way, side].astype(F32)
-
-    for side in range(2):
-        if side == 1:
+    def term_of(way, side, piece):
+        return b["terms"][way, side, piece * PIECE : (piece + 1) * PIECE, :]
+
+    def summed(step, way, side, piece):
+        hop(step - 1, way, side, piece).wait_recv()
+        return term_of(way, side, piece) + b["recv"][step - 1, way, side, piece].astype(F32)
+
+    places = [(side, piece, way) for side in range(2) for piece in range(2) for way in range(2)]
+    prepare(0, 0)
+    for side, piece, way in places:
+        if (side, piece, way) == (1, 0, 0):
             swap.wait()
-        for way in range(2):
-            b["send"][0, way, side] = partial(0, way, side).astype(BF)
-            hop(0, way, side).start()
+            prepare(0, 1)
+        b["send"][0, way, side, piece] = term_of(way, side, piece).astype(BF)
+        hop(0, way, side, piece).start()
 
     def one_step(step, carry):
-        for side in range(2):
-            for way in range(2):
-                b["send"][step, way, side] = summed(step, way, side).astype(BF)
-                hop(step, way, side).start()
+        prepare(step, 0)
+        prepare(step, 1)
+        for side, piece, way in places:
+            b["send"][step, way, side, piece] = summed(step, way, side, piece).astype(BF)
+            hop(step, way, side, piece).start()
         return carry
 
     lax.fori_loop(1, HEADS - 1, one_step, 0)
     final = HEADS - 1
-    for way in range(2):
-        b["own"][way * HALF : (way + 1) * HALF, :] = summed(final, way, 0)
+    prepare(final, 0)
+    prepare(final, 1)
     homes = []
-    for way in range(2):
-        rows = pl.ds(way * HALF, HALF)
-        b["home"][way * HALF : (way + 1) * HALF, :] = summed(final, way, 1).astype(BF)
-        homes.append(
-            copy(b["home"].at[rows], b["home_land"].at[rows], "home", way, "seq", partner)
-        )
+    for side, piece, way in places:
+        start = way * HALF + piece * PIECE
+        value = summed(final, way, side, piece)
+        if side == 0:
+            b["own"][start : start + PIECE, :] = value
+            continue
+        rows = pl.ds(start, PIECE)
+        b["home"][start : start + PIECE, :] = value.astype(BF)
+        at = 2 * way + piece
+        homes.append(copy(b["home"].at[rows], b["home_land"].at[rows], "home", at, "seq", partner))
         homes[-1].start()
     for one in squares:
         one.wait()
@@ -363,15 +428,13 @@
             out_ref[rows, i * N : (i + 1) * N] = (block * factor).astype(BF)
 
     def drain(step, carry):
-        for side in range(2):
-            for way in range(2):
-                hop(step, way, side).wait_send()
+        for side, piece, way in places:
+            hop(step, way, side, piece).wait_send()
         return carry
 
     lax.fori_loop(0, HEADS - 1, drain, 0)
-    for pair in moved:
-        for one in pair:
-            one.wait_send()
+    for one in sum(low + high, sideways):
+        one.wait_send()
 
 
 def body(
@@ -387,10 +450,6 @@
     out_weight,
     starts,
 ):
-    flags = jnp.broadcast_to(starts.astype(F32)[None, :], (8, TOK))
-    bias = jnp.broadcast_to(dt_bias[:, None], (HG, N))
-    logs = jnp.broadcast_to(a_log[:, None], (HG, N))
-    skip = jnp.broadcast_to(skip_d[:, None], (HG, P_SIZE)).reshape(1, WIDTH)
     sems = [pltpu.SemaphoreType.DMA(shape) for shape in SEMS.values()]
     return pl.pallas_call(
         layer_kernel,
@@ -401,8 +460,8 @@
         compiler_params=pltpu.CompilerParams(collective_id=0, has_side_effects=True),
         name="layer",
     )(
-        xbc, gate_z, dt_raw, bias, logs, skip, conv_weight, conv_bias[None, :],
-        norm_gain[None, :], out_weight.T, flags,
+        xbc, gate_z, dt_raw, dt_bias[None, :], a_log[None, :], skip_d[None, :], conv_weight,
+        conv_bias, norm_gain[None, :], out_weight.T, starts,
     )
 
 

time: 124 us -> 102 us (0.82)
  Pallas kernels: 117 us -> 99.8 us
  local copies, waits for them, and re-layouts: 6.43 us -> 1.77 us
    pallas_call x1, Pallas kernels: 117 us -> 99.8 us  [body(): pl.pallas_call(layer_kernel, out_shape=jax.ShapeDtypeStruct((TOK, 2 * COL...]
    broadcast_in_dim x5 -> x0, local copies, waits for them, and re-layouts: 3.3 us -> none  [the longest x1 1.31 us: body(): conv_bias[None, :]]
where the time goes in v4:
time: 102 us
  Pallas kernels  99.8 us (98%)
  local copies, waits for them, and re-layouts  1.77 us (2%)
    pallas_call x1, Pallas kernels, body(): pl.pallas_call(layer_kernel, out_shape=jax.ShapeDtypeStruct((TOK, 2 * COL...  99.8 us

profile of v4, /device:TPU:1, one launch (start us, length us, event | category | flops | bytes accessed | tf_op | source)
XLA Modules:
  0.0 101.6 jit_solution(15941950187868568822)
XLA Ops:
  0.0 99.8 %layer.1 = bf16[384,512]{1,0:T(8,128)(2,1)} custom-call(bf16[384,1280]{1,0:T(8,128)(2,1)} %xbc_ref.1, bf16[384,1024]{1,0:T(8,128)(2,1)} %gate_ref.1, bf16[16,384]{1,0:T(8,128)(2,1)} %dt_ref.1, f32[1,16]{1,0:T(1,128)} %bitcast.7, f32[1,16]{1,0:T(1,128)} %bitcast.8, f32[1,16]{1,0:T(1,128)} %bitcast.9, f32[4,1280]{1,0:T(4,128)} %taps_ref.1, f32[1280]{0:T(1024)} %shift_ref.1, ...), custom_call_target="tpu_custom_call" | custom-call | tf_op jit(solution)/shard_map/layer/pallas_call | solution.py:454
  99.8 1.8 %copy.13 = bf16[384,512]{1,0:T(8,128)(2,1)} copy(bf16[384,512]{1,0:T(8,128)(2,1)} %layer.1) | data formatting | bytes 786432

commit v5 on v4

--- a/solution.py
+++ b/solution.py
@@ -56,7 +56,7 @@
     home_land=((TOK, COLS), BF),
 )
 SEMS = dict(
-    halo=(2,), ax=(3,), az=(4, 2), bz=(4, 2), bx=(ROW, 3), rows=(7,), columns=(7,), backs=(7,),
+    halo=(2,), ax=(3,), az=(4, 2), bz=(4, 2), bx=(ROW, 4), rows=(7,), columns=(7,), backs=(7,),
     swap=(1,), ring=(HEADS - 1, 2, 2, 2), square=(7,), home=(4,),
 )
 
@@ -137,15 +137,30 @@
     block = pl.ds(pl.multiple_of(x * 64, 64), 64)
     halves = (pl.ds(0, WIDTH // 2), pl.ds(WIDTH // 2, WIDTH // 2))
     side_peers = [z * ROW + ((x + k) % 4) * 2 + core for k in range(1, 4)]
-    sideways = []
+
+    near = {}
+    far = []
 
     def fan(turn):
         chunk = (z + turn) % ROW
         part = b["weight_b"].at[chunk, block]
         source = weight_ref.at[:, halves[1]] if turn == 0 else part
-        for k, peer in enumerate(side_peers):
-            sideways.append(copy(source, part, "bx", (turn, k), "seq", peer))
-            sideways[-1].start()
+        near[turn] = [
+            copy(source, part, "bx", (turn, way), "seq", peer)
+            for way, peer in enumerate((side_peers[0], side_peers[2]))
+        ]
+        for one in near[turn]:
+            one.start()
+
+    def relay(turn):
+        chunk = (z + turn) % ROW
+        arrived(near[turn])
+        for way, peer in enumerate((side_peers[0], side_peers[2])):
+            source_x = (x + 3) % 4 if way == 0 else (x + 1) % 4
+            rows = pl.ds(pl.multiple_of(source_x * 64 + way * 32, 32), 32)
+            part = b["weight_b"].at[chunk, rows]
+            far.append(copy(part, part, "bx", (turn, 2 + way), "seq", peer))
+            far[-1].start()
 
     def pass_on(name, step):
         pair = []
@@ -214,6 +229,7 @@
     low.append(pass_on("bz", 2))
     fan(1)
     fan(7)
+    relay(0)
     for one in halo:
         one.wait()
     real = jnp.where(place > 0, 1.0, 0.0)
@@ -291,6 +307,8 @@
     b["column"][z] = b["total"][...]
     fan(2)
     fan(6)
+    relay(1)
+    relay(7)
     arrived(low[2])
     low.append(pass_on("bz", 4))
     fan(3)
@@ -318,6 +336,8 @@
     b["land"][j] = b["back"][j]
     arrived(low[3])
     fan(4)
+    for turn in (2, 6, 3, 5):
+        relay(turn)
     arrived(high[1])
     high.append(pass_on("az", 3))
     for one in copies:
@@ -348,8 +368,9 @@
         squares.append(copy(b["square"], b["squares"].at[h], "square", k, "head", peer))
         squares[-1].start()
     b["squares"][h] = b["square"][...]
+    relay(4)
     arrived(high[3])
-    arrived(sideways)
+    arrived(far)
     tokens = (b["gained"], b["other"])
 
     def prepare(step, side):
@@ -433,7 +454,7 @@
         return carry
 
     lax.fori_loop(0, HEADS - 1, drain, 0)
-    for one in sum(low + high, sideways):
+    for one in sum(low + high + list(near.values()), far):
         one.wait_send()
 
 

time: 102 us -> 100 us (0.980)
  Pallas kernels: 99.8 us -> 98.4 us
    pallas_call x1, Pallas kernels: 99.8 us -> 98.4 us  [body(): pl.pallas_call(layer_kernel, out_shape=jax.ShapeDtypeStruct((TOK, 2 * COL...]
where the time goes in v5:
time: 100 us
  Pallas kernels  98.4 us (98%)
  local copies, waits for them, and re-layouts  1.77 us (2%)
    pallas_call x1, Pallas kernels, body(): pl.pallas_call(layer_kernel, out_shape=jax.ShapeDtypeStruct((TOK, 2 * COL...  98.4 us

profile of v5, /device:TPU:1, one launch (start us, length us, event | category | flops | bytes accessed | tf_op | source)
XLA Modules:
  0.0 100.2 jit_solution(8095867689239893033)
XLA Ops:
  0.0 98.4 %layer.1 = bf16[384,512]{1,0:T(8,128)(2,1)} custom-call(bf16[384,1280]{1,0:T(8,128)(2,1)} %xbc_ref.1, bf16[384,1024]{1,0:T(8,128)(2,1)} %gate_ref.1, bf16[16,384]{1,0:T(8,128)(2,1)} %dt_ref.1, f32[1,16]{1,0:T(1,128)} %bitcast.7, f32[1,16]{1,0:T(1,128)} %bitcast.8, f32[1,16]{1,0:T(1,128)} %bitcast.9, f32[4,1280]{1,0:T(4,128)} %taps_ref.1, f32[1280]{0:T(1024)} %shift_ref.1, ...), custom_call_target="tpu_custom_call" | custom-call | tf_op jit(solution)/shard_map/layer/pallas_call | solution.py:475
  98.4 1.8 %copy.13 = bf16[384,512]{1,0:T(8,128)(2,1)} copy(bf16[384,512]{1,0:T(8,128)(2,1)} %layer.1) | data formatting | bytes 786432

commit v6 on v5

--- a/solution.py
+++ b/solution.py
@@ -14,6 +14,7 @@
 TOK = 384
 RIM = 16
 WIDTH = HG * P_SIZE
+SPLIT = 384
 PART = P_SIZE + 16
 ROW = 8
 HEADS = 8
@@ -42,8 +43,8 @@
     column=((ROW, 2, PART, N), BF),
     back=((ROW, 2, P_SIZE, N), BF),
     land=((ROW, 2, P_SIZE, N), BF),
-    weight_a=((HEADS, COLS, WIDTH // 2), BF),
-    weight_b=((HEADS, COLS, WIDTH // 2), BF),
+    weight_a=((HEADS, COLS, SPLIT), BF),
+    weight_b=((HEADS, COLS, WIDTH - SPLIT), BF),
     gained=((TOK, WIDTH), BF),
     other=((TOK, WIDTH), BF),
     send=((HEADS - 1, 2, 2, 2, PIECE, COLS), BF),
@@ -135,7 +136,7 @@
         )
 
     block = pl.ds(pl.multiple_of(x * 64, 64), 64)
-    halves = (pl.ds(0, WIDTH // 2), pl.ds(WIDTH // 2, WIDTH // 2))
+    halves = (pl.ds(0, SPLIT), pl.ds(SPLIT, WIDTH - SPLIT))
     side_peers = [z * ROW + ((x + k) % 4) * 2 + core for k in range(1, 4)]
 
     near = {}
@@ -204,8 +205,8 @@
         around[-1].start()
     low = [pass_on("bz", 1)]
     fan(0)
-    b["weight_a"][z, block] = weight_ref[:, : WIDTH // 2]
-    b["weight_b"][z, block] = weight_ref[:, WIDTH // 2 :]
+    b["weight_a"][z, block] = weight_ref[:, : SPLIT]
+    b["weight_b"][z, block] = weight_ref[:, SPLIT:]
     dt_col = columns_of(dt_ref[...].astype(F32)) + across(bias_ref)
     dt_col = jnp.maximum(dt_col, 0.0) + jnp.log1p(jnp.exp(-jnp.abs(dt_col)))
     log_col = -jnp.exp(across(log_ref)) * dt_col
@@ -377,8 +378,8 @@
         for way in range(2):
             chunk = (h + 2 * HEADS - 1 - step) % HEADS if way == 0 else (h + 1 + step) % HEADS
             rows = slice(way * HALF, (way + 1) * HALF)
-            term = dot(tokens[side][rows, : WIDTH // 2], b["weight_a"][chunk], 1, 1)
-            term = term + dot(tokens[side][rows, WIDTH // 2 :], b["weight_b"][chunk], 1, 1)
+            term = dot(tokens[side][rows, : SPLIT], b["weight_a"][chunk], 1, 1)
+            term = term + dot(tokens[side][rows, SPLIT:], b["weight_b"][chunk], 1, 1)
             b["terms"][way, side] = term
 
     def hop(step, way, side, piece):

time: 100 us -> 96.3 us (0.963)
  Pallas kernels: 98.4 us -> 94.3 us
    pallas_call x1, Pallas kernels: 98.4 us -> 94.3 us  [body(): pl.pallas_call(layer_kernel, out_shape=jax.ShapeDtypeStruct((TOK, 2 * COL...]
where the time goes in v6:
time: 96.3 us; the launch traced here: 96.1 us
  Pallas kernels  94.3 us (98%)
  local copies, waits for them, and re-layouts  1.77 us (2%)
    pallas_call x1, Pallas kernels, body(): pl.pallas_call(layer_kernel, out_shape=jax.ShapeDtypeStruct((TOK, 2 * COL...  94.3 us

profile of v6, /device:TPU:1, one launch (start us, length us, event | category | flops | bytes accessed | tf_op | source)
XLA Modules:
  0.0 96.1 jit_solution(10462205682797548049)
XLA Ops:
  0.0 94.3 %layer.1 = bf16[384,512]{1,0:T(8,128)(2,1)} custom-call(bf16[384,1280]{1,0:T(8,128)(2,1)} %xbc_ref.1, bf16[384,1024]{1,0:T(8,128)(2,1)} %gate_ref.1, bf16[16,384]{1,0:T(8,128)(2,1)} %dt_ref.1, f32[1,16]{1,0:T(1,128)} %bitcast.7, f32[1,16]{1,0:T(1,128)} %bitcast.8, f32[1,16]{1,0:T(1,128)} %bitcast.9, f32[4,1280]{1,0:T(4,128)} %taps_ref.1, f32[1280]{0:T(1024)} %shift_ref.1, ...), custom_call_target="tpu_custom_call" | custom-call | tf_op jit(solution)/shard_map/layer/pallas_call | solution.py:476
  94.3 1.8 %copy.13 = bf16[384,512]{1,0:T(8,128)(2,1)} copy(bf16[384,512]{1,0:T(8,128)(2,1)} %layer.1) | data formatting | bytes 786432
